TPU v7x, 128 devices: a whole 4x4x4 slice. The times are simulated.
128 devices in a mesh: sec: 2 (over core), blk: 64 (over z, x, y).
Axes of the slice: x: 4, y: 4, z: 4, core: 2. Of those that a mesh axis runs over, the one named last changes fastest.
Arguments:
- state: float32 [2, 4, 16, 131072], P('sec', None, None, 'blk'), may hold values from -6 to 6
- neighbour: int32 [2, 6, 131072], P('sec', None, 'blk'), may hold values from 0 to 2303, as said below
- edge_weight: float32 [2, 6, 131072], P('sec', None, 'blk'), may hold values from 0.02 to 0.15
- coupling_rate: float32 [2, 4, 131072], P('sec', None, 'blk'), may hold values from 0.05 to 0.5
- vertical_mix: float32 [2, 4, 16, 16], P('sec'), may hold values from -1 to 2, as said below
- remap_source: int32 [2, 524288], P('sec', 'blk'), may hold values from 0 to 2047
- remap_owner: int32 [2, 524288, 1], P('sec', 'blk'), may hold values from 0 to 63; in each aligned block of 8192 rows (0 to 8191, 8192 to 16383, ..., all dimensions but the last counted through in order) at most 256 rows name the same one
- remap_cell: int32 [2, 524288], P('sec', 'blk'), may hold values from 0 to 2047
- remap_weight: float32 [2, 524288], P('sec', 'blk'), may hold values from 0.1 to 0.6
Outputs:
- new_state: float32 [2, 4, 16, 131072], P('sec', None, None, 'blk')
- remapped: float32 [2, 4, 131072], P('sec', None, 'blk')
Inputs may be any that keep to these rules, and one draw needn't show every extreme that they name: Entry (s, k, c) is the position of neighbour k of cell c in c's block extended by 128 cells on each side: positions below 128 are the previous block's last cells, then the own block, then the next block's first cells; blocks wrap around. `vertical_mix`: each inverse is an identity-dominated dense matrix. `remap_source`: entries of a block name source cells of that same block. `remap_owner`: among the 8192 rows of one block no destination block is named by more than 256 rows; some block names one destination exactly 256 times.
All inputs are finite; a program needn't handle non-finite values.
Results may differ from a plain program's by a relative error of at most 0.0001.
Values sent between devices are 32-bit elements; how exact they have to be, the bound alone decides.
No kernel may reach another device: no remote copies, remote signals or barrier semaphores. Data moves between devices by JAX's collectives and lax.ppermute only.
A program may use at most 128 MiB of HBM per device.

v0:
```python
import jax
import jax.numpy as jnp
from jax import lax
from jax.sharding import PartitionSpec as P

SUB = 4


def swapped(x, axis, bit):
    return lax.ppermute(x, axis, [(i, i ^ 1 << bit) for i in range(lax.axis_size(axis))])


def with_halo(block, sides, width):
    for axis, dim in sides:
        count = lax.axis_size(axis)
        forward = [(i, i + 1) for i in range(count - 1)]
        forward.append((count - 1, 0))
        backward = [(target, source) for source, target in forward]
        low = lax.ppermute(
            lax.slice_in_dim(block, block.shape[dim] - width, None, axis=dim), axis, forward
        )
        high = lax.ppermute(lax.slice_in_dim(block, 0, width, axis=dim), axis, backward)
        block = jnp.concatenate([low, block, high], axis=dim)
    return block


def per_device(
    state,
    neighbour,
    edge_weight,
    coupling_rate,
    vertical_mix,
    remap_source,
    remap_owner,
    remap_cell,
    remap_weight,
):
    fields = state[0]
    num_fields = fields.shape[0]
    levels = fields.shape[1]
    block_cells = fields.shape[2]
    columns = num_fields * levels
    slots = neighbour.shape[1]
    blocks = lax.axis_size("blk")
    entry_count = remap_source.shape[1]
    capacity = 2 * entry_count // blocks
    reach = block_cells // 16
    surface = fields[:, 0, :]
    values = remap_weight[0][None, :] * jnp.take(surface, remap_source[0], axis=1)
    owners = remap_owner[0, :, 0]
    counts = jnp.sum(
        (owners[:, None] == jnp.arange(blocks, dtype=jnp.int32)[None, :]).astype(jnp.int32), axis=0
    )
    starts = jnp.cumsum(counts) - counts
    ordering = jnp.argsort(owners, stable=True)
    sorted_owner = owners[ordering]
    slot_index = (
        sorted_owner * capacity + jnp.arange(entry_count, dtype=jnp.int32) - starts[sorted_owner]
    )
    packed = (
        jnp.zeros((num_fields, blocks * capacity), jnp.float32)
        .at[:, slot_index]
        .set(values[:, ordering])
    )
    packed = packed.reshape(num_fields, blocks, capacity)
    targets = (
        jnp.zeros((blocks * capacity,), jnp.float32)
        .at[slot_index]
        .set(remap_cell[0][ordering].astype(jnp.float32))
    )
    targets = targets.reshape(1, blocks, capacity)
    packed, targets = (
        lax.all_to_all(packed, "blk", split_axis=1, concat_axis=1, tiled=True),
        lax.all_to_all(targets, "blk", split_axis=1, concat_axis=1, tiled=True),
    )
    packed, targets = swapped((packed, targets), "sec", 0)
    dest_cells = targets.reshape(-1).astype(jnp.int32)
    remapped = (
        jnp.zeros((num_fields, block_cells), jnp.float32)
        .at[:, dest_cells]
        .add(packed.reshape(num_fields, -1))
    )
    cell_rows = fields.reshape(columns, block_cells).T
    weights = edge_weight[0].T[:, :, None]
    flat_lists = neighbour[0].T.reshape(-1)
    mixed_rows = cell_rows
    for step in range(SUB):
        extended = with_halo(mixed_rows, (("blk", 0),), reach)
        taken = jnp.take(extended, flat_lists, axis=0).reshape(block_cells, slots, columns)
        update = jnp.sum(weights * (taken - mixed_rows[:, None, :]), axis=1)
        mixed_rows = mixed_rows + update
    mixed = mixed_rows.T.reshape(num_fields, levels, block_cells)
    surface_top = mixed[:, 0, :] + coupling_rate[0] * (remapped - mixed[:, 0, :])
    forced = mixed.at[:, 0, :].set(surface_top)
    result = jnp.einsum("fij,fjc->fic", vertical_mix[0], forced, precision=lax.Precision.HIGHEST)
    return (result[None], remapped[None])


def solution(mesh):
    return jax.shard_map(
        per_device,
        mesh=mesh,
        in_specs=(
            P("sec", None, None, "blk"),
            P("sec", None, "blk"),
            P("sec", None, "blk"),
            P("sec", None, "blk"),
            P("sec", None, None, None),
            P("sec", "blk"),
            P("sec", "blk", None),
            P("sec", "blk"),
            P("sec", "blk"),
        ),
        out_specs=(P("sec", None, None, "blk"), P("sec", None, "blk")),
        check_vma=False,
    )
```

profile of v0, /device:TPU:65, one launch (start us, length us, event | category | flops | bytes accessed | tf_op | source)
XLA Modules:
  0.0 785.2 jit_solution(1050114154603726388)
XLA Ops:
  19.0 45.7 %gather_fusion = s32[8192]{0:T(1024)S(1)} fusion(s32[8192]{0:T(1024)S(1)} %bitcast.138, s32[8192]{0:T(1024)S(1)} %fusion.8), kind=kCustom, calls=%fused_computation.4 | custom fusion | bytes 98304 | tf_op jit(solution)/shard_map/gather | solution.py:56
  74.9 36.0 %select_select_fusion = s32[8192]{0:T(1024)S(1)} fusion(pred[8192]{0:T(1024)(128)(4,1)S(1)} %get-tuple-element.81, pred[8192]{0:T(1024)(128)(4,1)S(1)} %get-tuple-element.80, pred[8192]{0:T(1024)(128)(4,1)S(1)} %get-tuple-element.79, pred[8192]{0:T(1024)(128)(4,1)S(1)} %get-tuple-element.78, pred[8192]{0:T(1024)(128)(4,1)S(1)} %get-tuple-element.77, ...), kind=kLoop, calls=%fused_computation.115 | loop fusion | flops 466944 | bytes 532708 | tf_op jit(solution)/shard_map/gather | solution.py:58
  111.1 45.5 %gather_fusion.1 = s32[8192]{0:T(1024)S(1)} fusion(s32[8192]{0:T(1024)S(1)} %bitcast.139, s32[8192]{0:T(1024)S(1)} %fusion.8), kind=kCustom, calls=%fused_computation.5 | custom fusion | bytes 98304 | tf_op jit(solution)/shard_map/gather | solution.py:69
  156.7 31.0 %scatter_custom_fusion = f32[16384]{0:T(1024)} fusion(s32[8192]{0:T(1024)S(1)} %bitcast.164, f32[8192]{0:T(1024)S(1)} %convert_element_type.20, f32[]{:T(128)} %constant.63.clone.1), kind=kCustom, calls=%fused_computation.116 | custom fusion | bytes 65540 | tf_op jit(solution)/shard_map/scatter | solution.py:69
  187.7 12.7 %all-to-all-start = ((f32[1,64,256]{2,0,1:T(1,128)}), f32[1,64,256]{2,0,1:T(1,128)}, u32[]{:S(2)}, u32[]{:S(2)}) async-start(f32[1,64,256]{2,0,1:T(1,128)} %bitcast.82), calls=%async_computation | async-start | bytes 131072 | tf_op jit(solution)/shard_map/all_to_all | solution.py:74
  201.6 8.5 %copy.53 = f32[1,4,16,2048]{1,3,2,0:T(8,128)} copy(f32[1,4,16,2048]{3,2,1,0:T(8,128)S(1)} %copy-done.16) | data formatting | bytes 1048576 | tf_op args[0]
  213.8 41.0 %gather_fusion.3 = f32[12288,64]{1,0:T(8,128)} fusion(f32[2304,64]{1,0:T(8,128)S(1)} %pad_maximum_fusion, s32[12288]{0:T(1024)S(1)} %fusion.7), kind=kCustom, calls=%fused_computation.clone | custom fusion | bytes 6340608 | tf_op jit(solution)/shard_map/jit(_take)/gather | solution.py:89
  254.8 10.3 %broadcast_select_fusion.3 = f32[12288,64]{1,0:T(8,128)} fusion(f32[12288,64]{1,0:T(8,128)} %gather_fusion.3, pred[12288]{0:T(1024)(128)(4,1)S(1)} %compare_and_fusion), kind=kLoop, calls=%fused_computation.22 | loop fusion | flops 786432 | bytes 6303744 | tf_op jit(solution)/shard_map/jit(_take)/select_n | solution.py:89
  273.5 12.9 %multiply_reduce_fusion.3 = f32[2048,64]{1,0:T(8,128)S(1)} fusion(f32[2048,6,64]{2,1,0:T(8,128)} %reshape.200, f32[2048,64]{1,0:T(8,128)S(1)} %bitcast.143, f32[2048,6]{1,0:T(8,128)S(1)} %bitcast.144), kind=kLoop, calls=%fused_computation.14 | loop fusion | flops 2228224 | bytes 4243456 | tf_op jit(solution)/shard_map/reduce_sum | solution.py:90
  292.3 27.7 %gather_fusion.2 = f32[8192,4]{1,0:T(8,128)} fusion(f32[4,2048]{0,1:T(8,128)S(1)} %copy-done.13, s32[8192]{0:T(1024)S(1)} %broadcast_clamp_fusion), kind=kCustom, calls=%fused_computation.6 | custom fusion | bytes 294912 | tf_op jit(solution)/shard_map/jit(_take)/gather | solution.py:49
  321.3 41.0 %gather_fusion.4 = f32[12288,64]{1,0:T(8,128)} fusion(f32[2304,64]{1,0:T(8,128)S(1)} %pad_maximum_fusion.1, s32[12288]{0:T(1024)S(1)} %fusion.7), kind=kCustom, calls=%fused_computation.1.clone | custom fusion | bytes 6340608 | tf_op jit(solution)/shard_map/jit(_take)/gather | solution.py:89
  362.4 10.3 %broadcast_select_fusion.2 = f32[12288,64]{1,0:T(8,128)} fusion(f32[12288,64]{1,0:T(8,128)} %gather_fusion.4, pred[12288]{0:T(1024)(128)(4,1)S(1)} %compare_and_fusion), kind=kLoop, calls=%fused_computation.21 | loop fusion | flops 786432 | bytes 6303744 | tf_op jit(solution)/shard_map/jit(_take)/select_n | solution.py:89
  372.7 8.4 %reshape.201 = f32[2048,6,64]{2,1,0:T(8,128)} reshape(f32[12288,64]{1,0:T(8,128)} %broadcast_select_fusion.2) | data formatting | bytes 6291456 | tf_op jit(solution)/shard_map/reshape | solution.py:89
  381.1 13.0 %multiply_reduce_fusion.2 = f32[2048,64]{1,0:T(8,128)S(1)} fusion(f32[2048,6,64]{2,1,0:T(8,128)} %reshape.201, f32[2048,64]{1,0:T(8,128)S(1)} %copy-done.6, f32[2048,6]{1,0:T(8,128)S(1)} %bitcast.145), kind=kLoop, calls=%fused_computation.13 | loop fusion | flops 2228224 | bytes 4243456 | tf_op jit(solution)/shard_map/reduce_sum | solution.py:90
  408.0 70.3 %scatter_custom_fusion.1 = f32[4,16384]{0,1:T(8,128)} fusion(s32[8192]{0:T(1024)} %bitcast.165, f32[4,8192]{0,1:T(8,128)} %multiply_bitcast_fusion, s32[8192]{0:T(1024)S(1)} %fusion.8, f32[]{:T(128)} %constant.63.clone.1), kind=kCustom, calls=%fused_computation.16 | custom fusion | bytes 262656 | tf_op jit(solution)/shard_map/scatter | solution.py:63
  484.2 12.8 %all-to-all-start.1 = ((f32[4,64,256]{2,0,1:T(4,128)}), f32[4,64,256]{2,0,1:T(4,128)}, u32[]{:S(2)}, u32[]{:S(2)}) async-start(f32[4,64,256]{2,0,1:T(4,128)} %copy.54), calls=%async_computation.1 | async-start | bytes 524288 | tf_op jit(solution)/shard_map/all_to_all | solution.py:73
  501.9 41.0 %gather_fusion.5 = f32[12288,64]{1,0:T(8,128)} fusion(f32[2304,64]{1,0:T(8,128)S(1)} %pad_maximum_fusion.2, s32[12288]{0:T(1024)S(1)} %fusion.7), kind=kCustom, calls=%fused_computation.2.clone | custom fusion | bytes 6340608 | tf_op jit(solution)/shard_map/jit(_take)/gather | solution.py:89
  542.9 10.3 %broadcast_select_fusion.1 = f32[12288,64]{1,0:T(8,128)} fusion(f32[12288,64]{1,0:T(8,128)} %gather_fusion.5, pred[12288]{0:T(1024)(128)(4,1)S(1)} %compare_and_fusion), kind=kLoop, calls=%fused_computation.20 | loop fusion | flops 786432 | bytes 6303744 | tf_op jit(solution)/shard_map/jit(_take)/select_n | solution.py:89
  553.3 8.4 %reshape.202 = f32[2048,6,64]{2,1,0:T(8,128)} reshape(f32[12288,64]{1,0:T(8,128)} %broadcast_select_fusion.1) | data formatting | bytes 6291456 | tf_op jit(solution)/shard_map/reshape | solution.py:89
  561.7 12.8 %multiply_reduce_fusion.1 = f32[2048,64]{1,0:T(8,128)S(1)} fusion(f32[2048,6,64]{2,1,0:T(8,128)} %reshape.202, f32[2048,64]{1,0:T(8,128)S(1)} %copy-done.4, f32[2048,6]{1,0:T(8,128)S(1)} %bitcast.146), kind=kLoop, calls=%fused_computation.12 | loop fusion | flops 2228224 | bytes 4243456 | tf_op jit(solution)/shard_map/reduce_sum | solution.py:90
  586.7 41.2 %gather_fusion.6 = f32[12288,64]{1,0:T(8,128)} fusion(f32[2304,64]{1,0:T(8,128)S(1)} %pad_maximum_fusion.3, s32[12288]{0:T(1024)S(1)} %fusion.7), kind=kCustom, calls=%fused_computation.3.clone | custom fusion | bytes 6340608 | tf_op jit(solution)/shard_map/jit(_take)/gather | solution.py:89
  627.9 10.3 %broadcast_select_fusion = f32[12288,64]{1,0:T(8,128)} fusion(f32[12288,64]{1,0:T(8,128)} %gather_fusion.6, pred[12288]{0:T(1024)(128)(4,1)S(1)} %compare_and_fusion), kind=kLoop, calls=%fused_computation.19 | loop fusion | flops 786432 | bytes 6303744 | tf_op jit(solution)/shard_map/jit(_take)/select_n | solution.py:89
  646.7 13.8 %multiply_reduce_fusion = f32[2048,64]{1,0:T(8,128)} fusion(f32[2048,6,64]{2,1,0:T(8,128)} %reshape.203, f32[2048,64]{1,0:T(8,128)S(1)} %copy-done.8, f32[2048,6]{1,0:T(8,128)S(1)} %bitcast.147), kind=kLoop, calls=%fused_computation.11 | loop fusion | flops 2228224 | bytes 4243456 | tf_op jit(solution)/shard_map/reduce_sum | solution.py:90
  672.4 104.8 %scatter_custom_fusion.2 = f32[4,2048]{0,1:T(8,128)S(1)} fusion(s32[16384]{0:T(1024)S(1)} %bitcast.162, f32[16384,4]{1,0:T(8,128)} %bitcast.150, f32[]{:T(128)} %constant.63.clone.1), kind=kCustom, calls=%fused_computation.39 | custom fusion | flops 65536 | bytes 33280 | tf_op jit(solution)/shard_map/scatter-add | solution.py:81
  (123 shorter events, 113.5 us)
Async XLA Ops:
  0.6 782.0 %copy-start = (f32[1,4,16,16]{3,2,1,0:T(8,128)S(1)}, f32[1,4,16,16]{3,2,1,0:T(8,128)}, u32[]{:S(2)}) copy-start(f32[1,4,16,16]{3,2,1,0:T(8,128)} %param.17) | copy-start | bytes 12292
  0.6 18.3 %copy-start.1 = (s32[1,8192,1]{1,2,0:T(1,128)S(1)}, s32[1,8192,1]{1,2,0:T(1,128)}, u32[]{:S(2)}) copy-start(s32[1,8192,1]{1,2,0:T(1,128)} %param.19) | copy-start | bytes 98308
  2.7 210.2 %collective-permute-start.1 = (f32[128,64]{1,0:T(8,128)}, f32[128,64]{1,0:T(8,128)S(1)}, u32[]{:S(2)}, u32[]{:S(2)}) collective-permute-start(f32[128,64]{1,0:T(8,128)} %get-tuple-element.91), channel_id=1, source_target_pairs={{1,0},{2,1},{3,2},{4,3},{5,4},{6,5},{7,6},{8,7},{9,8},{10,9},{11,1... | collective-permute-start | bytes 98312 | tf_op jit(solution)/shard_map/ppermute | solution.py:22
  7.2 205.7 %collective-permute-start = (f32[128,64]{1,0:T(8,128)S(1)}, f32[128,64]{1,0:T(8,128)}, u32[]{:S(2)}, u32[]{:S(2)}) collective-permute-start(f32[128,64]{1,0:T(8,128)S(1)} %get-tuple-element.90), channel_id=1, source_target_pairs={{0,1},{1,2},{2,3},{3,4},{4,5},{5,6},{6,7},{7,8},{8,9},{9,10},{10,1... | collective-permute-start | bytes 98312 | tf_op jit(solution)/shard_map/ppermute | solution.py:19
  64.7 46.4 %copy-start.2 = (s32[1,8192]{1,0:T(1,128)S(1)}, s32[1,8192]{1,0:T(1,128)}, u32[]{:S(2)}) copy-start(s32[1,8192]{1,0:T(1,128)} %param.20) | copy-start | bytes 98308
  111.1 45.6 %copy-start.22 = (s32[8192,1]{0,1:T(1,128)}, s32[8192,1]{0,1:T(1,128)S(1)}, u32[]{:S(2)}) copy-start(s32[8192,1]{0,1:T(1,128)S(1)} %compare_select_fusion.2) | copy-start | bytes 98308
  111.1 89.3 %copy-start.18 = (s32[1,6,2048]{2,0,1:T(1,128)S(1)}, s32[1,6,2048]{2,0,1:T(1,128)}, u32[]{:S(2)}) copy-start(s32[1,6,2048]{2,0,1:T(1,128)} %param.14) | copy-start | bytes 147460
  111.1 90.5 %copy-start.16 = (f32[1,4,16,2048]{3,2,1,0:T(8,128)S(1)}, f32[1,4,16,2048]{3,2,1,0:T(8,128)}, u32[]{:S(2)}) copy-start(f32[1,4,16,2048]{3,2,1,0:T(8,128)} %param.13) | copy-start | bytes 1572868
  187.7 296.5 %all-to-all-start = ((f32[1,64,256]{2,0,1:T(1,128)}), f32[1,64,256]{2,0,1:T(1,128)}, u32[]{:S(2)}, u32[]{:S(2)}) async-start(f32[1,64,256]{2,0,1:T(1,128)} %bitcast.82), calls=%async_computation | async-start | bytes 131072 | tf_op jit(solution)/shard_map/all_to_all | solution.py:74
  273.5 18.7 %copy-start.13 = (f32[4,2048]{0,1:T(8,128)S(1)}, f32[4,2048]{0,1:T(8,128)}, u32[]{:S(2)}) copy-start(f32[4,2048]{0,1:T(8,128)} %slice_bitcast_fusion) | copy-start | bytes 98308
  287.7 32.2 %collective-permute-start.3 = (f32[128,64]{1,0:T(8,128)S(1)}, f32[128,64]{1,0:T(8,128)S(1)}, u32[]{:S(2)}, u32[]{:S(2)}) collective-permute-start(f32[128,64]{1,0:T(8,128)S(1)} %get-tuple-element.89), channel_id=1, source_target_pairs={{1,0},{2,1},{3,2},{4,3},{5,4},{6,5},{7,6},{8,7},{9,8},{10,9},{11,1... | collective-permute-start | bytes 98312 | tf_op jit(solution)/shard_map/ppermute | solution.py:22
  292.2 27.7 %collective-permute-start.2 = (f32[128,64]{1,0:T(8,128)S(1)}, f32[128,64]{1,0:T(8,128)}, u32[]{:S(2)}, u32[]{:S(2)}) collective-permute-start(f32[128,64]{1,0:T(8,128)S(1)} %get-tuple-element.88), channel_id=1, source_target_pairs={{0,1},{1,2},{2,3},{3,4},{4,5},{5,6},{6,7},{7,8},{8,9},{9,10},{10,1... | collective-permute-start | bytes 98312 | tf_op jit(solution)/shard_map/ppermute | solution.py:19
  381.1 20.1 %copy-start.12 = (f32[8192,4]{1,0:T(8,128)S(1)}, f32[8192,4]{1,0:T(8,128)}, u32[]{:S(2)}) copy-start(f32[8192,4]{1,0:T(8,128)} %gather_fusion.2) | copy-start | bytes 393220
  381.1 20.1 %copy-start.20 = (f32[1,8192]{1,0:T(1,128)S(1)}, f32[1,8192]{1,0:T(1,128)}, u32[]{:S(2)}) copy-start(f32[1,8192]{1,0:T(1,128)} %param.21) | copy-start | bytes 98308
  394.1 12.5 %copy-start.21 = (f32[1,4,2048]{2,1,0:T(4,128)S(1)}, f32[1,4,2048]{2,1,0:T(4,128)}, u32[]{:S(2)}) copy-start(f32[1,4,2048]{2,1,0:T(4,128)} %param.16) | copy-start | bytes 98308
  395.5 105.1 %collective-permute-start.5 = (f32[128,64]{1,0:T(8,128)S(1)}, f32[128,64]{1,0:T(8,128)S(1)}, u32[]{:S(2)}, u32[]{:S(2)}) collective-permute-start(f32[128,64]{1,0:T(8,128)S(1)} %get-tuple-element.87), channel_id=1, source_target_pairs={{1,0},{2,1},{3,2},{4,3},{5,4},{6,5},{7,6},{8,7},{9,8},{10,9},{11,1... | collective-permute-start | bytes 98312 | tf_op jit(solution)/shard_map/ppermute | solution.py:22
  401.2 99.4 %collective-permute-start.4 = (f32[128,64]{1,0:T(8,128)S(1)}, f32[128,64]{1,0:T(8,128)S(1)}, u32[]{:S(2)}, u32[]{:S(2)}) collective-permute-start(f32[128,64]{1,0:T(8,128)S(1)} %get-tuple-element.86), channel_id=1, source_target_pairs={{0,1},{1,2},{2,3},{3,4},{4,5},{5,6},{6,7},{7,8},{8,9},{9,10},{10,1... | collective-permute-start | bytes 98312 | tf_op jit(solution)/shard_map/ppermute | solution.py:19
  484.2 176.3 %all-to-all-start.1 = ((f32[4,64,256]{2,0,1:T(4,128)}), f32[4,64,256]{2,0,1:T(4,128)}, u32[]{:S(2)}, u32[]{:S(2)}) async-start(f32[4,64,256]{2,0,1:T(4,128)} %copy.54), calls=%async_computation.1 | async-start | bytes 524288 | tf_op jit(solution)/shard_map/all_to_all | solution.py:73
  497.0 82.3 %collective-permute-start.8 = (f32[1,64,256]{2,0,1:T(1,128)}, f32[1,64,256]{2,0,1:T(1,128)}, u32[]{:S(2)}, u32[]{:S(2)}) collective-permute-start(f32[1,64,256]{2,0,1:T(1,128)} %all-to-all-done), channel_id=1, source_target_pairs={{0,64},{64,0},{1,65},{65,1},{2,66},{66,2},{3,67},{67,3},{4,68},{68... | collective-permute-start | bytes 196616 | tf_op jit(solution)/shard_map/ppermute | solution.py:10
  574.7 11.9 %copy-start.7 = (f32[2048,64]{1,0:T(8,128)}, f32[2048,64]{1,0:T(8,128)S(1)}, u32[]{:S(2)}) copy-start(f32[2048,64]{1,0:T(8,128)S(1)} %add.113) | copy-start | bytes 1572868
  574.7 5.9 collective-permute-start.7
  579.3 7.3 collective-permute-start.6
  662.2 5.4 collective-permute-start.9
  666.1 111.0 %copy-start.14 = (f32[1,4,2048]{1,2,0:T(8,128)S(1)}, f32[1,4,2048]{1,2,0:T(8,128)}, u32[]{:S(2)}) copy-start(f32[1,4,2048]{1,2,0:T(8,128)} %copy.51) | copy-start | bytes 98308
  (11 other events, 58.9 us)
where the time goes:
time: 794 us; the launch traced here: 785 us
  local copies, waits for them, and re-layouts  457 us (58%)
  other arithmetic  268 us (34%)
  starting transfers between devices  49.8 us (6%)
    gather x4, local copies, waits for them, and re-layouts, per_device(): jnp.take(extended, flat_lists, axis=0).reshape(block_cells, slots, columns)  164 us
    scatter-add x1, other arithmetic, per_device(): remapped = jnp.zeros((num_fields, block_cells), jnp.float32).at[:, dest_c...  105 us
    scatter x1, local copies, waits for them, and re-layouts, per_device(): packed = jnp.zeros((num_fields, blocks * capacity), jnp.float32).at[:, sl...  70.3 us
    reduce_sum x4, other arithmetic, per_device(): update = jnp.sum(weights * (taken - mixed_rows[:, None, :]), axis=1)  52.5 us
    gather x3, other arithmetic, per_device(): starts[sorted_owner]  46.3 us
    gather x1, local copies, waits for them, and re-layouts, per_device(): sorted_owner = owners[ordering]  45.7 us
    gather x1, local copies, waits for them, and re-layouts, per_device(): remap_cell[0][ordering].astype(jnp.float32)  45.5 us
    select_n x4, other arithmetic, per_device(): jnp.take(extended, flat_lists, axis=0).reshape(block_cells, slots, columns)  41.4 us
  transfers between devices with their start and end apart: 12, of which 2 were waited for; matrix products, arithmetic and copies ran while one was open for 77% of the time, Pallas kernels for 0%

commit v1 on v0

v1 whole, which is shorter than its diff:
```python
import jax
import jax.numpy as jnp
from jax import lax
from jax.experimental import pallas as pl
from jax.experimental.pallas import tpu as pltpu
from jax.sharding import PartitionSpec as P

SUB = 4
RIM = 128
LANE = 128
BF = jnp.bfloat16
F32 = jnp.float32
VMEM = pltpu.VMEM


def dot(a, b):
    return jnp.dot(a, b, preferred_element_type=F32)


def dot_nt(a, b):
    return lax.dot_general(a, b, (((1,), (1,)), ((), ())), preferred_element_type=F32)


def split(x):
    hi = x.astype(BF)
    lo = (x - hi.astype(F32)).astype(BF)
    return hi, lo


def build_kernel(nbr_ref, w_ref, hi_ref, lo_ref, diag_ref):
    slots, width = nbr_ref.shape
    rows = hi_ref.shape[0]
    cells = rows - 2 * RIM
    pos, wgt = [], []
    for k in range(slots):
        p = nbr_ref[k : k + 1, :]
        p = jnp.where(p < RIM, p + cells, jnp.where(p < cells + RIM, p - RIM, p))
        pos.append(p)
        wgt.append(w_ref[k : k + 1, :])
    total = wgt[0]
    for k in range(1, slots):
        total = total + wgt[k]
    diag_ref[...] = 1.0 - total
    for k in range(1, slots):
        for j in range(k):
            same = pos[j] == pos[k]
            wgt[j] = jnp.where(same, wgt[j] + wgt[k], wgt[j])
            pos[k] = jnp.where(same, -1, pos[k])
    step = 32
    whi, wlo = [], []
    for k in range(slots):
        hi = wgt[k].astype(BF).astype(F32)
        whi.append(jnp.broadcast_to(hi, (step, width)).astype(BF))
        wlo.append(jnp.broadcast_to(wgt[k] - hi, (step, width)).astype(BF))
    for block in range(rows // 256):
        loc = []
        for k in range(slots):
            local = pos[k] - block * 256
            local = jnp.where((local >= 0) & (local < 256), local, -1).astype(F32)
            loc.append(jnp.broadcast_to(local, (step, width)).astype(BF))
        for part in range(256 // step):
            row = (lax.broadcasted_iota(jnp.int32, (step, width), 0) + part * step).astype(F32).astype(BF)
            hi = jnp.zeros((step, width), BF)
            lo = jnp.zeros((step, width), BF)
            for k in range(slots):
                here = row == loc[k]
                hi = jnp.where(here, whi[k], hi)
                lo = jnp.where(here, wlo[k], lo)
            at = pl.ds(block * 256 + part * step, step)
            hi_ref[at, :] = hi
            lo_ref[at, :] = lo


def build(nbr, w):
    slots, cells = nbr.shape
    rows = cells + 2 * RIM
    width = 128
    return pl.pallas_call(
        build_kernel,
        grid=(cells // width,),
        in_specs=[pl.BlockSpec((slots, width), lambda i: (0, i))] * 2,
        out_specs=[
            pl.BlockSpec((rows, width), lambda i: (0, i)),
            pl.BlockSpec((rows, width), lambda i: (0, i)),
            pl.BlockSpec((1, width), lambda i: (0, i)),
        ],
        out_shape=[
            jax.ShapeDtypeStruct((rows, cells), BF),
            jax.ShapeDtypeStruct((rows, cells), BF),
            jax.ShapeDtypeStruct((1, cells), F32),
        ],
        name="build",
    )(nbr, w)


def own_kernel(x_ref, hi_ref, lo_ref, diag_ref, out_ref, cat_ref):
    columns = x_ref.shape[0]
    width = out_ref.shape[1]

    @pl.when(pl.program_id(0) == 0)
    def _():
        hi, lo = split(x_ref[...])
        cat_ref[0:columns, :] = hi
        cat_ref[columns:, :] = lo

    both = dot(cat_ref[...], hi_ref[...])
    low = dot(cat_ref[0:columns, :], lo_ref[...])
    at = pl.ds(pl.multiple_of(pl.program_id(0) * width, width), width)
    out_ref[...] = diag_ref[...] * x_ref[:, at] + (both[0:columns] + both[columns:] + low)


def own(x, a_hi, a_lo, diag):
    columns, cells = x.shape
    width = 256
    return pl.pallas_call(
        own_kernel,
        grid=(cells // width,),
        in_specs=[
            pl.BlockSpec((columns, cells), lambda i: (0, 0)),
            pl.BlockSpec((cells, width), lambda i: (0, i)),
            pl.BlockSpec((cells, width), lambda i: (0, i)),
            pl.BlockSpec((1, width), lambda i: (0, i)),
        ],
        out_specs=pl.BlockSpec((columns, width), lambda i: (0, i)),
        out_shape=jax.ShapeDtypeStruct((columns, cells), F32),
        scratch_shapes=[VMEM((2 * columns, cells), BF)],
        name="own",
    )(x, a_hi, a_lo, diag)


def rim_update(part, low_ref, high_ref, hi_ref, lo_ref):
    columns = low_ref.shape[0]
    lo_hi, lo_lo = split(low_ref[...])
    hi_hi, hi_lo = split(high_ref[...])
    top = jnp.concatenate([lo_hi, hi_hi], axis=1)
    rest = jnp.concatenate([lo_lo, hi_lo], axis=1)
    both = dot(jnp.concatenate([top, rest], axis=0), hi_ref[...])
    return part + (both[0:columns] + both[columns:] + dot(top, lo_ref[...]))


def rim_kernel(part_ref, low_ref, high_ref, hi_ref, lo_ref, out_ref, first_ref, last_ref):
    out = rim_update(part_ref[...], low_ref, high_ref, hi_ref, lo_ref)
    out_ref[...] = out
    first_ref[...] = out[:, 0:RIM]
    last_ref[...] = out[:, out.shape[1] - RIM :]


def rim(part, low, high, a_hi, a_lo):
    columns, cells = part.shape
    last = cells // (2 * RIM)
    return pl.pallas_call(
        rim_kernel,
        grid=(1,),
        in_specs=[
            pl.BlockSpec((columns, cells), lambda i: (0, 0)),
            pl.BlockSpec((columns, RIM), lambda i: (0, 0)),
            pl.BlockSpec((columns, RIM), lambda i: (0, 0)),
            pl.BlockSpec((2 * RIM, cells), lambda i: (last, 0)),
            pl.BlockSpec((2 * RIM, cells), lambda i: (last, 0)),
        ],
        out_specs=[
            pl.BlockSpec((columns, cells), lambda i: (0, 0)),
            pl.BlockSpec((columns, RIM), lambda i: (0, 0)),
            pl.BlockSpec((columns, RIM), lambda i: (0, 0)),
        ],
        out_shape=[
            jax.ShapeDtypeStruct((columns, cells), F32),
            jax.ShapeDtypeStruct((columns, RIM), F32),
            jax.ShapeDtypeStruct((columns, RIM), F32),
        ],
        name="rim",
    )(part, low, high, a_hi, a_lo)


def finish_kernel(
    part_ref, low_ref, high_ref, hi_ref, lo_ref, remapped_ref, rate_ref, mix_ref, out_ref
):
    mixed = rim_update(part_ref[...], low_ref, high_ref, hi_ref, lo_ref)
    fields, levels = mix_ref.shape[0], mix_ref.shape[1]
    for f in range(fields):
        own_levels = mixed[f * levels : (f + 1) * levels]
        top = own_levels[0:1]
        top = top + rate_ref[f : f + 1, :] * (remapped_ref[f : f + 1, :] - top)
        row = lax.broadcasted_iota(jnp.int32, own_levels.shape, 0)
        forced = jnp.where(row == 0, jnp.broadcast_to(top, own_levels.shape), own_levels)
        out_ref[f] = jnp.dot(
            mix_ref[f], forced, preferred_element_type=F32, precision=lax.Precision.HIGHEST
        )


def finish(part, low, high, a_hi, a_lo, remapped, rate, mix):
    columns, cells = part.shape
    fields, levels = mix.shape[0], mix.shape[1]
    last = cells // (2 * RIM)
    return pl.pallas_call(
        finish_kernel,
        grid=(1,),
        in_specs=[
            pl.BlockSpec((columns, cells), lambda i: (0, 0)),
            pl.BlockSpec((columns, RIM), lambda i: (0, 0)),
            pl.BlockSpec((columns, RIM), lambda i: (0, 0)),
            pl.BlockSpec((2 * RIM, cells), lambda i: (last, 0)),
            pl.BlockSpec((2 * RIM, cells), lambda i: (last, 0)),
            pl.BlockSpec((fields, cells), lambda i: (0, 0)),
            pl.BlockSpec((fields, cells), lambda i: (0, 0)),
            pl.BlockSpec((fields, levels, levels), lambda i: (0, 0, 0)),
        ],
        out_specs=pl.BlockSpec((fields, levels, cells), lambda i: (0, 0, 0)),
        out_shape=jax.ShapeDtypeStruct((fields, levels, cells), F32),
        name="finish",
    )(part, low, high, a_hi, a_lo, remapped, rate, mix)


def pack_kernel(
    surface_ref, source_ref, owner_ref, cell_ref, weight_ref,
    vals_ref, cells_ref,
    tiles_ref, half_ref, slot_ref, hot_ref, left_ref, cleft_ref, right_ref, acc_ref, cacc_ref,
):
    fields = surface_ref.shape[0]
    rows = source_ref.shape[0]
    blocks = cells_ref.shape[0] // 2
    chunk = right_ref.shape[1]
    per = chunk // LANE
    source = source_ref[...]
    line, lane = source // LANE, source % LANE
    vals = []
    for f in range(fields):
        got = jnp.zeros((rows, LANE), F32)
        for h in range(surface_ref.shape[1] // LANE):
            table = jnp.broadcast_to(surface_ref[f : f + 1, h * LANE : (h + 1) * LANE], (rows, LANE))
            one = jnp.take_along_axis(table, lane, axis=1, mode="promise_in_bounds")
            got = jnp.where(line == h, one, got)
        vals.append(got * weight_ref[...])
    owner_row = lax.broadcasted_iota(jnp.int32, (blocks, LANE), 0)
    i0 = lax.broadcasted_iota(jnp.int32, (LANE, LANE), 0)
    i1 = lax.broadcasted_iota(jnp.int32, (LANE, LANE), 1)
    before = (i0 < i1).astype(F32).astype(BF)
    for r in range(rows):
        hot = (owner_row == owner_ref[r : r + 1, :]).astype(F32)
        hot_ref[r * blocks : (r + 1) * blocks, :] = hot.astype(BF)
    prefix = dot(hot_ref[...], before)
    base = jnp.zeros((blocks, 1), F32)
    for r in range(rows):
        hot = hot_ref[r * blocks : (r + 1) * blocks, :].astype(F32)
        rank = jnp.sum(hot * (prefix[r * blocks : (r + 1) * blocks] + base), axis=0, keepdims=True)
        slot_ref[r : r + 1, :] = rank.astype(jnp.int32)
        base = base + jnp.sum(hot, axis=1, keepdims=True)
    slot = slot_ref[...]
    half = slot // LANE
    slot_ref[...] = slot % LANE
    for h in range(2):
        for f in range(fields):
            tiles_ref[pl.ds(h * fields + f, rows, stride=2 * fields), :] = jnp.where(
                half == h, vals[f], 0.0
            )
    cell = cell_ref[...]
    for part, piece in enumerate(((cell // 16) * 16, cell % 16)):
        for h in range(2):
            half_ref[pl.ds(part * 2 + h, rows, stride=4), :] = jnp.where(
                half == h, piece, 0
            ).astype(F32)

    acc_ref[...] = jnp.zeros_like(acc_ref)
    cacc_ref[...] = jnp.zeros_like(cacc_ref)

    def body(c, _):
        for t in range(per):
            r = c * per + t
            at = pl.ds(t * LANE, LANE)
            tile = tiles_ref[pl.ds(pl.multiple_of(r * 8, 8), 8), :]
            hi = tile.astype(BF).astype(F32)
            tile = jnp.concatenate([hi, tile - hi], axis=0).astype(BF)
            who = jnp.broadcast_to(owner_ref[pl.ds(r, 1), :].astype(F32), (16, LANE)).astype(BF)
            zero = jnp.zeros((16, LANE), BF)
            for o in range(blocks):
                left_ref[o * 16 : (o + 1) * 16, at] = jnp.where(who == o, tile, zero)
            who = jnp.broadcast_to(owner_ref[pl.ds(r, 1), :], (2 * blocks, LANE))
            row = lax.broadcasted_iota(jnp.int32, (2 * blocks, LANE), 0)
            for part in range(2):
                a = jnp.broadcast_to(half_ref[pl.ds(r * 4 + part * 2, 1), :], (2 * blocks, LANE))
                b = jnp.broadcast_to(half_ref[pl.ds(r * 4 + part * 2 + 1, 1), :], (2 * blocks, LANE))
                picked = jnp.where(row % 2 == 0, a, b)
                cleft_ref[part * 2 * blocks : (part + 1) * 2 * blocks, at] = jnp.where(
                    row // 2 == who, picked, 0.0
                ).astype(BF)
            lanes = jnp.broadcast_to(slot_ref[pl.ds(r, 1), :], (LANE, LANE))
            right_ref[:, at] = (i0 == lanes).astype(F32).astype(BF)
        acc_ref[...] += dot_nt(left_ref[...], right_ref[...])
        cacc_ref[...] += dot_nt(cleft_ref[...], right_ref[...])
        return 0

    lax.fori_loop(0, rows // per, body, 0)
    for o in range(blocks):
        vals_ref[o * 8 : (o + 1) * 8, :] = acc_ref[o * 16 : o * 16 + 8, :] + acc_ref[o * 16 + 8 : o * 16 + 16, :]
    cells_ref[...] = cacc_ref[0 : 2 * blocks, :] + cacc_ref[2 * blocks :, :]


def pack(surface, source, owner, cell, weight, blocks):
    fields = surface.shape[0]
    rows = source.shape[0]
    chunk = 512
    return pl.pallas_call(
        pack_kernel,
        in_specs=[pl.BlockSpec(memory_space=VMEM)] * 5,
        out_specs=[pl.BlockSpec(memory_space=VMEM)] * 2,
        out_shape=[
            jax.ShapeDtypeStruct((blocks * 8, LANE), F32),
            jax.ShapeDtypeStruct((blocks * 2, LANE), F32),
        ],
        scratch_shapes=[
            VMEM((rows * 2 * fields, LANE), F32),
            VMEM((rows * 4, LANE), F32),
            VMEM((rows, LANE), jnp.int32),
            VMEM((rows * blocks, LANE), BF),
            VMEM((blocks * 16, chunk), BF),
            VMEM((blocks * 4, chunk), BF),
            VMEM((LANE, chunk), BF),
            VMEM((blocks * 16, LANE), F32),
            VMEM((blocks * 4, LANE), F32),
        ],
        name="pack",
    )(surface, source, owner, cell, weight)


def unpack_kernel(vals_ref, cells_ref, out_ref, left_ref, right_ref):
    fields, cells = out_ref.shape
    rows = cells_ref.shape[0]
    groups = cells // 256
    chunk = right_ref.shape[1]
    per = chunk // LANE
    r256 = lax.broadcasted_iota(jnp.int32, (256, LANE), 0)

    def body(c, acc):
        for t in range(per):
            r = c * per + t
            at = pl.ds(t * LANE, LANE)
            cell = cells_ref[pl.ds(r, 1), :].astype(jnp.int32)
            group, local = cell // 256, cell % 256
            vals = vals_ref[pl.ds(pl.multiple_of(r * fields, fields), fields), :]
            hi = vals.astype(BF).astype(F32)
            tile = jnp.concatenate([hi, vals - hi], axis=0)
            for g in range(groups):
                picked = jnp.where(jnp.broadcast_to(group, tile.shape) == g, tile, 0.0)
                left_ref[g * 8 : (g + 1) * 8, at] = picked
            right_ref[:, at] = (r256 == jnp.broadcast_to(local, (256, LANE))).astype(F32).astype(BF)
        return acc + dot_nt(left_ref[...].astype(BF), right_ref[...])

    acc = lax.fori_loop(0, rows // per, body, jnp.zeros((groups * 8, 256), F32))
    for g in range(groups):
        out_ref[:, g * 256 : (g + 1) * 256] = (
            acc[g * 8 : g * 8 + fields] + acc[g * 8 + fields : g * 8 + 2 * fields]
        )


def unpack(vals, cells, count):
    fields = vals.shape[0] // cells.shape[0]
    chunk = 1024
    return pl.pallas_call(
        unpack_kernel,
        in_specs=[pl.BlockSpec(memory_space=VMEM)] * 2,
        out_specs=pl.BlockSpec(memory_space=VMEM),
        out_shape=jax.ShapeDtypeStruct((fields, count), F32),
        scratch_shapes=[
            VMEM((count // 256 * 8, chunk), F32),
            VMEM((256, chunk), BF),
        ],
        name="unpack",
    )(vals, cells)


def per_device(
    state, neighbour, edge_weight, coupling_rate, vertical_mix,
    remap_source, remap_owner, remap_cell, remap_weight,
):
    fields, levels, cells = state.shape[1:]
    columns = fields * levels
    blocks = lax.axis_size("blk")
    forward = [(i, (i + 1) % blocks) for i in range(blocks)]
    backward = [(b, a) for a, b in forward]

    def lines(x):
        return x.reshape(-1, LANE)

    def exchange(first, last):
        low = lax.ppermute(last, "blk", forward)
        high = lax.ppermute(first, "blk", backward)
        return low, high

    x = state.reshape(columns, cells)
    halo = exchange(x[:, :RIM], x[:, cells - RIM :])
    vals, dest = pack(
        state[0, :, 0, :], lines(remap_source), lines(remap_owner), lines(remap_cell),
        lines(remap_weight), blocks,
    )
    vals = lax.all_to_all(vals.reshape(blocks, 8, LANE), "blk", 0, 0, tiled=True).reshape(-1, LANE)
    dest = lax.all_to_all(dest.reshape(blocks, 2, LANE), "blk", 0, 0, tiled=True).reshape(-1, LANE)
    a_hi, a_lo, diag = build(neighbour[0], edge_weight[0])
    for step in range(SUB - 1):
        part = own(x, a_hi, a_lo, diag)
        x, first, last = rim(part, *halo, a_hi, a_lo)
        halo = exchange(first, last)
    part = own(x, a_hi, a_lo, diag)
    partial_sum = unpack(vals, dest, cells)
    remapped = lax.ppermute(partial_sum, "sec", [(0, 1), (1, 0)])
    out = finish(part, *halo, a_hi, a_lo, remapped, coupling_rate[0], vertical_mix[0])
    return out[None], remapped[None]


def solution(mesh):
    return jax.shard_map(
        per_device,
        mesh=mesh,
        in_specs=(
            P("sec", None, None, "blk"),
            P("sec", None, "blk"),
            P("sec", None, "blk"),
            P("sec", None, "blk"),
            P("sec", None, None, None),
            P("sec", "blk"),
            P("sec", "blk", None),
            P("sec", "blk"),
            P("sec", "blk"),
        ),
        out_specs=(P("sec", None, None, "blk"), P("sec", None, "blk")),
        check_vma=False,
    )
```

time: 794 us -> 160 us (0.20)
  the two profiles are of different devices: /device:TPU:65 before, /device:TPU:1 now
where the time goes in v1:
time: 160 us; the launch traced here: 158 us
  Pallas kernels  88.9 us (56%)
  starting transfers between devices  36.2 us (23%)
  blocking collectives  20.7 us (13%)
  local copies, waits for them, and re-layouts  11.6 us (7%)
    pallas_call x4, Pallas kernels, own(): pl.pallas_call(own_kernel, grid=(cells // width,), in_specs=[pl.BlockSpec...  42.1 us
    ppermute x4, starting transfers between devices, exchange(): high = lax.ppermute(first, 'blk', backward)  26.6 us
    all_to_all x1, blocking collectives, per_device(): lax.all_to_all(dest.reshape(blocks, 2, LANE), 'blk', 0, 0, tiled=True)  20.7 us
    pallas_call x1, Pallas kernels, build(): pl.pallas_call(build_kernel, grid=(cells // width,), in_specs=[pl.BlockSp...  13.6 us
    pallas_call x1, Pallas kernels, pack(): pl.pallas_call(pack_kernel, in_specs=[pl.BlockSpec(memory_space=VMEM)] *...  12.8 us
    unnamed x24, local copies, waits for them, and re-layouts  9.86 us
    pallas_call x3, Pallas kernels, rim(): pl.pallas_call(rim_kernel, grid=(1,), in_specs=[pl.BlockSpec((columns, ce...  8.97 us
    pallas_call x1, Pallas kernels, unpack(): pl.pallas_call(unpack_kernel, in_specs=[pl.BlockSpec(memory_space=VMEM)]...  7.68 us
  transfers between devices with their start and end apart: 10, of which 0 were waited for; matrix products, arithmetic and copies ran while one was open for 2% of the time, Pallas kernels for 41%

profile of v1, /device:TPU:1, one launch (start us, length us, event | category | flops | bytes accessed | tf_op | source)
XLA Modules:
  0.0 158.2 jit_solution(2113508064371343414)
XLA Ops:
  0.6 1.0 slice.11
  2.2 12.8 %pack.1 = (f32[512,128]{1,0:T(8,128)}, f32[128,128]{1,0:T(8,128)}) custom-call(f32[4,2048]{1,0:T(4,128)} %bitcast.31, s32[64,128]{1,0:T(8,128)} %bitcast.35, s32[64,128]{1,0:T(8,128)} %bitcast.36, s32[64,128]{1,0:T(8,128)} %bitcast.37, f32[64,128]{1,0:T(8,128)} %bitcast.38), custom_call_target="tpu_custom_call" | custom-call | tf_op jit(solution)/shard_map/pack/pallas_call | solution.py:302
  15.0 20.7 %all_to_all.10 = f32[64,2,128]{2,1,0:T(2,128)} all-to-all(f32[64,2,128]{2,1,0:T(2,128)} %bitcast.32), channel_id=1, replica_groups=mesh['sec'=2,'blk'=64] {'blk'}, dimensions={0} | all-to-all | bytes 131072 | tf_op jit(solution)/shard_map/all_to_all | solution.py:396
  35.7 5.0 %all-to-all-start = ((f32[64,8,128]{2,1,0:T(8,128)}), f32[64,8,128]{2,1,0:T(8,128)S(1)}, u32[]{:S(2)}, u32[]{:S(2)}) async-start(f32[64,8,128]{2,1,0:T(8,128)} %bitcast.28), calls=%async_computation | async-start | bytes 524288 | tf_op jit(solution)/shard_map/all_to_all | solution.py:395
  40.7 0.8 fusion
  41.4 1.0 collective-permute-start
  42.4 5.9 %collective-permute-start.1 = (f32[64,128]{1,0:T(8,128)S(1)}, f32[64,128]{1,0:T(8,128)S(1)}, u32[]{:S(2)}, u32[]{:S(2)}) collective-permute-start(f32[64,128]{1,0:T(8,128)S(1)} %get-tuple-element.30), channel_id=1, source_target_pairs={{1,0},{2,1},{3,2},{4,3},{5,4},{6,5},{7,6},{8,7},{9,8},{10,9},{11,1... | collective-permute-start | bytes 98312 | tf_op jit(solution)/shard_map/ppermute | solution.py:386
  48.3 1.5 copy.18
  49.8 1.4 copy.19
  51.2 13.6 %build.1 = (bf16[2304,2048]{1,0:T(8,128)(2,1)}, bf16[2304,2048]{1,0:T(8,128)(2,1)}, f32[1,2048]{1,0:T(1,128)}) custom-call(s32[6,2048]{1,0:T(8,128)} %bitcast.27, f32[6,2048]{1,0:T(8,128)} %bitcast.26), custom_call_target="tpu_custom_call" | custom-call | tf_op jit(solution)/shard_map/build/pallas_call | solution.py:78
  64.8 10.5 %own.4.part_ref = f32[64,2048]{1,0:T(8,128)} custom-call(f32[64,2048]{1,0:T(8,128)} %bitcast.24, bf16[2304,2048]{1,0:T(8,128)(2,1)} %get-tuple-element.16.hi_ref, bf16[2304,2048]{1,0:T(8,128)(2,1)} %get-tuple-element.17.lo_ref, f32[1,2048]{1,0:T(1,128)} %get-tuple-element.18.diag_ref), custom_call_target="tpu_custom_call" | custom-call | tf_op jit(solution)/shard_map/own/pallas_call | solution.py:115
  76.6 3.0 %rim.3 = (f32[64,2048]{1,0:T(8,128)}, f32[64,128]{1,0:T(8,128)}, f32[64,128]{1,0:T(8,128)}) custom-call(f32[64,2048]{1,0:T(8,128)} %own.4.part_ref, f32[64,128]{1,0:T(8,128)} %copy-done.2, f32[64,128]{1,0:T(8,128)} %copy-done.3, bf16[2304,2048]{1,0:T(8,128)(2,1)} %get-tuple-element.16.hi_ref, bf16[2304,2048]{1,0:T(8,128)(2,1)} %get-tuple-element.17.lo_ref), custom_call_target="tpu_custom_call" | custom-call | tf_op jit(solution)/shard_map/rim/pallas_call | solution.py:151
  79.6 6.9 %collective-permute-start.3 = (f32[64,128]{1,0:T(8,128)}, f32[64,128]{1,0:T(8,128)S(1)}, u32[]{:S(2)}, u32[]{:S(2)}) collective-permute-start(f32[64,128]{1,0:T(8,128)} %get-tuple-element.21), channel_id=1, source_target_pairs={{1,0},{2,1},{3,2},{4,3},{5,4},{6,5},{7,6},{8,7},{9,8},{10,9},{11,1... | collective-permute-start | bytes 98312 | tf_op jit(solution)/shard_map/ppermute | solution.py:386
  86.5 10.5 %own.5.part_ref = f32[64,2048]{1,0:T(8,128)} custom-call(f32[64,2048]{1,0:T(8,128)} %get-tuple-element.19.x_ref, bf16[2304,2048]{1,0:T(8,128)(2,1)} %get-tuple-element.16.hi_ref, bf16[2304,2048]{1,0:T(8,128)(2,1)} %get-tuple-element.17.lo_ref, f32[1,2048]{1,0:T(1,128)} %get-tuple-element.18.diag_ref), custom_call_target="tpu_custom_call" | custom-call | tf_op jit(solution)/shard_map/own/pallas_call | solution.py:115
  98.2 3.0 %rim.4 = (f32[64,2048]{1,0:T(8,128)}, f32[64,128]{1,0:T(8,128)}, f32[64,128]{1,0:T(8,128)}) custom-call(f32[64,2048]{1,0:T(8,128)} %own.5.part_ref, f32[64,128]{1,0:T(8,128)} %copy-done.6, f32[64,128]{1,0:T(8,128)} %copy-done.8, bf16[2304,2048]{1,0:T(8,128)(2,1)} %get-tuple-element.16.hi_ref, bf16[2304,2048]{1,0:T(8,128)(2,1)} %get-tuple-element.17.lo_ref), custom_call_target="tpu_custom_call" | custom-call | tf_op jit(solution)/shard_map/rim/pallas_call | solution.py:151
  101.2 6.9 %collective-permute-start.5 = (f32[64,128]{1,0:T(8,128)}, f32[64,128]{1,0:T(8,128)S(1)}, u32[]{:S(2)}, u32[]{:S(2)}) collective-permute-start(f32[64,128]{1,0:T(8,128)} %get-tuple-element.24), channel_id=1, source_target_pairs={{1,0},{2,1},{3,2},{4,3},{5,4},{6,5},{7,6},{8,7},{9,8},{10,9},{11,1... | collective-permute-start | bytes 98312 | tf_op jit(solution)/shard_map/ppermute | solution.py:386
  108.1 10.5 %own.6.part_ref = f32[64,2048]{1,0:T(8,128)} custom-call(f32[64,2048]{1,0:T(8,128)} %get-tuple-element.22.x_ref, bf16[2304,2048]{1,0:T(8,128)(2,1)} %get-tuple-element.16.hi_ref, bf16[2304,2048]{1,0:T(8,128)(2,1)} %get-tuple-element.17.lo_ref, f32[1,2048]{1,0:T(1,128)} %get-tuple-element.18.diag_ref), custom_call_target="tpu_custom_call" | custom-call | tf_op jit(solution)/shard_map/own/pallas_call | solution.py:115
  119.9 3.0 %rim.5 = (f32[64,2048]{1,0:T(8,128)}, f32[64,128]{1,0:T(8,128)}, f32[64,128]{1,0:T(8,128)}) custom-call(f32[64,2048]{1,0:T(8,128)} %own.6.part_ref, f32[64,128]{1,0:T(8,128)} %copy-done.7, f32[64,128]{1,0:T(8,128)} %copy-done.9, bf16[2304,2048]{1,0:T(8,128)(2,1)} %get-tuple-element.16.hi_ref, bf16[2304,2048]{1,0:T(8,128)(2,1)} %get-tuple-element.17.lo_ref), custom_call_target="tpu_custom_call" | custom-call | tf_op jit(solution)/shard_map/rim/pallas_call | solution.py:151
  123.6 7.7 %unpack.1 = f32[4,2048]{1,0:T(4,128)} custom-call(f32[512,128]{1,0:T(8,128)} %bitcast.22, f32[128,128]{1,0:T(8,128)} %bitcast.29), custom_call_target="tpu_custom_call" | custom-call | tf_op jit(solution)/shard_map/unpack/pallas_call | solution.py:358
  131.3 3.7 %collective-permute-start.8 = (f32[4,2048]{1,0:T(4,128)}, f32[4,2048]{1,0:T(4,128)S(1)}, u32[]{:S(2)}, u32[]{:S(2)}) collective-permute-start(f32[4,2048]{1,0:T(4,128)} %unpack.1), channel_id=1, source_target_pairs={{0,64},{64,0},{1,65},{65,1},{2,66},{66,2},{3,67},{67,3},{4,68},{68... | collective-permute-start | bytes 98312 | tf_op jit(solution)/shard_map/ppermute | solution.py:404
  134.9 6.9 %collective-permute-start.7 = (f32[64,128]{1,0:T(8,128)}, f32[64,128]{1,0:T(8,128)S(1)}, u32[]{:S(2)}, u32[]{:S(2)}) collective-permute-start(f32[64,128]{1,0:T(8,128)} %get-tuple-element.27), channel_id=1, source_target_pairs={{1,0},{2,1},{3,2},{4,3},{5,4},{6,5},{7,6},{8,7},{9,8},{10,9},{11,1... | collective-permute-start | bytes 98312 | tf_op jit(solution)/shard_map/ppermute | solution.py:386
  141.8 10.5 %own.7.part_ref = f32[64,2048]{1,0:T(8,128)} custom-call(f32[64,2048]{1,0:T(8,128)} %get-tuple-element.25.x_ref, bf16[2304,2048]{1,0:T(8,128)(2,1)} %get-tuple-element.16.hi_ref, bf16[2304,2048]{1,0:T(8,128)(2,1)} %get-tuple-element.17.lo_ref, f32[1,2048]{1,0:T(1,128)} %get-tuple-element.18.diag_ref), custom_call_target="tpu_custom_call" | custom-call | tf_op jit(solution)/shard_map/own/pallas_call | solution.py:115
  153.0 3.8 %finish.1 = f32[4,16,2048]{2,1,0:T(8,128)} custom-call(f32[64,2048]{1,0:T(8,128)} %own.7.part_ref, f32[64,128]{1,0:T(8,128)} %copy-done.4, f32[64,128]{1,0:T(8,128)} %copy-done.5, bf16[2304,2048]{1,0:T(8,128)(2,1)} %get-tuple-element.16.hi_ref, bf16[2304,2048]{1,0:T(8,128)(2,1)} %get-tuple-element.17.lo_ref, f32[4,2048]{1,0:T(4,128)} %copy-done.1, ...), custom_call_target="tpu_custom_call" | custom-call | tf_op jit(solution)/shard_map/finish/pallas_call | solution.py:195
  156.8 1.4 copy.22
  (34 shorter events, 5.6 us)
Async XLA Ops:
  35.7 87.2 %all-to-all-start = ((f32[64,8,128]{2,1,0:T(8,128)}), f32[64,8,128]{2,1,0:T(8,128)S(1)}, u32[]{:S(2)}, u32[]{:S(2)}) async-start(f32[64,8,128]{2,1,0:T(8,128)} %bitcast.28), calls=%async_computation | async-start | bytes 524288 | tf_op jit(solution)/shard_map/all_to_all | solution.py:395
  41.4 33.9 %collective-permute-start = (f32[64,128]{1,0:T(8,128)S(1)}, f32[64,128]{1,0:T(8,128)S(1)}, u32[]{:S(2)}, u32[]{:S(2)}) collective-permute-start(f32[64,128]{1,0:T(8,128)S(1)} %get-tuple-element.31), channel_id=1, source_target_pairs={{0,1},{1,2},{2,3},{3,4},{4,5},{5,6},{6,7},{7,8},{8,9},{9,10},{10,1... | collective-permute-start | bytes 98312 | tf_op jit(solution)/shard_map/ppermute | solution.py:385
  42.4 32.9 %collective-permute-start.1 = (f32[64,128]{1,0:T(8,128)S(1)}, f32[64,128]{1,0:T(8,128)S(1)}, u32[]{:S(2)}, u32[]{:S(2)}) collective-permute-start(f32[64,128]{1,0:T(8,128)S(1)} %get-tuple-element.30), channel_id=1, source_target_pairs={{1,0},{2,1},{3,2},{4,3},{5,4},{6,5},{7,6},{8,7},{9,8},{10,9},{11,1... | collective-permute-start | bytes 98312 | tf_op jit(solution)/shard_map/ppermute | solution.py:386
  75.4 0.6 copy-start.2
  76.0 0.6 copy-start.3
  79.6 17.4 %collective-permute-start.2 = (f32[64,128]{1,0:T(8,128)}, f32[64,128]{1,0:T(8,128)S(1)}, u32[]{:S(2)}, u32[]{:S(2)}) collective-permute-start(f32[64,128]{1,0:T(8,128)} %get-tuple-element.20), channel_id=1, source_target_pairs={{0,1},{1,2},{2,3},{3,4},{4,5},{5,6},{6,7},{7,8},{8,9},{9,10},{10,1... | collective-permute-start | bytes 98312 | tf_op jit(solution)/shard_map/ppermute | solution.py:385
  79.6 17.4 %collective-permute-start.3 = (f32[64,128]{1,0:T(8,128)}, f32[64,128]{1,0:T(8,128)S(1)}, u32[]{:S(2)}, u32[]{:S(2)}) collective-permute-start(f32[64,128]{1,0:T(8,128)} %get-tuple-element.21), channel_id=1, source_target_pairs={{1,0},{2,1},{3,2},{4,3},{5,4},{6,5},{7,6},{8,7},{9,8},{10,9},{11,1... | collective-permute-start | bytes 98312 | tf_op jit(solution)/shard_map/ppermute | solution.py:386
  97.0 0.6 copy-start.6
  97.6 0.6 copy-start.8
  101.2 17.4 %collective-permute-start.4 = (f32[64,128]{1,0:T(8,128)}, f32[64,128]{1,0:T(8,128)S(1)}, u32[]{:S(2)}, u32[]{:S(2)}) collective-permute-start(f32[64,128]{1,0:T(8,128)} %get-tuple-element.23), channel_id=1, source_target_pairs={{0,1},{1,2},{2,3},{3,4},{4,5},{5,6},{6,7},{7,8},{8,9},{9,10},{10,1... | collective-permute-start | bytes 98312 | tf_op jit(solution)/shard_map/ppermute | solution.py:385
  101.2 17.4 %collective-permute-start.5 = (f32[64,128]{1,0:T(8,128)}, f32[64,128]{1,0:T(8,128)S(1)}, u32[]{:S(2)}, u32[]{:S(2)}) collective-permute-start(f32[64,128]{1,0:T(8,128)} %get-tuple-element.24), channel_id=1, source_target_pairs={{1,0},{2,1},{3,2},{4,3},{5,4},{6,5},{7,6},{8,7},{9,8},{10,9},{11,1... | collective-permute-start | bytes 98312 | tf_op jit(solution)/shard_map/ppermute | solution.py:386
  118.7 0.6 copy-start.7
  119.3 0.6 copy-start.9
  122.9 0.7 copy-start
  131.3 21.1 %collective-permute-start.8 = (f32[4,2048]{1,0:T(4,128)}, f32[4,2048]{1,0:T(4,128)S(1)}, u32[]{:S(2)}, u32[]{:S(2)}) collective-permute-start(f32[4,2048]{1,0:T(4,128)} %unpack.1), channel_id=1, source_target_pairs={{0,64},{64,0},{1,65},{65,1},{2,66},{66,2},{3,67},{67,3},{4,68},{68... | collective-permute-start | bytes 98312 | tf_op jit(solution)/shard_map/ppermute | solution.py:404
  134.9 17.4 %collective-permute-start.6 = (f32[64,128]{1,0:T(8,128)}, f32[64,128]{1,0:T(8,128)S(1)}, u32[]{:S(2)}, u32[]{:S(2)}) collective-permute-start(f32[64,128]{1,0:T(8,128)} %get-tuple-element.26), channel_id=1, source_target_pairs={{0,1},{1,2},{2,3},{3,4},{4,5},{5,6},{6,7},{7,8},{8,9},{9,10},{10,1... | collective-permute-start | bytes 98312 | tf_op jit(solution)/shard_map/ppermute | solution.py:385
  134.9 17.5 %collective-permute-start.7 = (f32[64,128]{1,0:T(8,128)}, f32[64,128]{1,0:T(8,128)S(1)}, u32[]{:S(2)}, u32[]{:S(2)}) collective-permute-start(f32[64,128]{1,0:T(8,128)} %get-tuple-element.27), channel_id=1, source_target_pairs={{1,0},{2,1},{3,2},{4,3},{5,4},{6,5},{7,6},{8,7},{9,8},{10,9},{11,1... | collective-permute-start | bytes 98312 | tf_op jit(solution)/shard_map/ppermute | solution.py:386
  152.4 0.6 copy-start.1
  152.4 0.6 copy-start.4
  152.4 0.6 copy-start.5

commit v2 on v0

v2 whole, which is shorter than its diff:
```python
import jax
import jax.numpy as jnp
from jax import lax
from jax.experimental import pallas as pl
from jax.experimental.pallas import tpu as pltpu
from jax.sharding import PartitionSpec as P

SUB = 4
RIM = 128
LANE = 128
BF = jnp.bfloat16
F32 = jnp.float32
VMEM = pltpu.VMEM


def dot(a, b):
    return jnp.dot(a, b, preferred_element_type=F32)


def dot_nt(a, b):
    return lax.dot_general(a, b, (((1,), (1,)), ((), ())), preferred_element_type=F32)


def split(x):
    hi = x.astype(BF)
    lo = (x - hi.astype(F32)).astype(BF)
    return hi, lo


def build_kernel(nbr_ref, w_ref, hi_ref, lo_ref, diag_ref):
    rows, cells = hi_ref.shape
    lines = cells // LANE
    slots = nbr_ref.shape[0] // lines
    step = 16
    first = lax.broadcasted_iota(jnp.int32, (step, LANE), 0).astype(F32)

    def body(i, _):
        lanes = pl.ds(pl.multiple_of(i * LANE, LANE), LANE)
        pos, wgt = [], []
        for k in range(slots):
            p = nbr_ref[pl.ds(k * lines + i, 1), :]
            p = jnp.where(p < RIM, p + cells, jnp.where(p < cells + RIM, p - RIM, p))
            pos.append(p)
            wgt.append(w_ref[pl.ds(k * lines + i, 1), :])
        total = wgt[0]
        for k in range(1, slots):
            total = total + wgt[k]
        diag_ref[:, lanes] = 1.0 - total
        for k in range(1, slots):
            for j in range(k):
                same = pos[j] == pos[k]
                wgt[j] = jnp.where(same, wgt[j] + wgt[k], wgt[j])
                pos[k] = jnp.where(same, -1, pos[k])
        whi, wlo = [], []
        for k in range(slots):
            hi = wgt[k].astype(BF).astype(F32)
            whi.append(jnp.broadcast_to(hi, (step, LANE)).astype(BF))
            wlo.append(jnp.broadcast_to(wgt[k] - hi, (step, LANE)).astype(BF))
        for block in range(rows // 256):
            loc = []
            for k in range(slots):
                local = pos[k] - block * 256
                local = jnp.where((local >= 0) & (local < 256), local, -1).astype(F32)
                loc.append(jnp.broadcast_to(local, (step, LANE)).astype(BF))
            for part in range(256 // step):
                row = (first + part * step).astype(BF)
                hi = jnp.zeros((step, LANE), BF)
                lo = jnp.zeros((step, LANE), BF)
                for k in range(slots):
                    here = row == loc[k]
                    hi = jnp.where(here, whi[k], hi)
                    lo = jnp.where(here, wlo[k], lo)
                at = pl.ds(block * 256 + part * step, step)
                hi_ref[at, lanes] = hi
                lo_ref[at, lanes] = lo
        return 0

    lax.fori_loop(0, lines, body, 0)


def params(mb):
    return pltpu.CompilerParams(vmem_limit_bytes=mb << 20)


def whole(count):
    return [pl.BlockSpec(memory_space=VMEM)] * count


def build(nbr, w, cells):
    rows = cells + 2 * RIM
    return pl.pallas_call(
        build_kernel,
        in_specs=whole(2),
        out_specs=whole(3),
        out_shape=[
            jax.ShapeDtypeStruct((rows, cells), BF),
            jax.ShapeDtypeStruct((rows, cells), BF),
            jax.ShapeDtypeStruct((1, cells), F32),
        ],
        compiler_params=params(24),
        name="build",
    )(nbr, w)


def own_kernel(x_ref, hi_ref, lo_ref, diag_ref, out_ref, cat_ref):
    columns, cells = x_ref.shape
    hi, lo = split(x_ref[...])
    cat_ref[0:columns, :] = hi
    cat_ref[columns:, :] = lo
    for c in range(cells // 256):
        at = pl.ds(c * 256, 256)
        both = dot(cat_ref[...], hi_ref[0:cells, at])
        low = dot(cat_ref[0:columns, :], lo_ref[0:cells, at])
        out_ref[:, at] = diag_ref[:, at] * x_ref[:, at] + (both[0:columns] + both[columns:] + low)


def own(x, a_hi, a_lo, diag):
    columns, cells = x.shape
    return pl.pallas_call(
        own_kernel,
        in_specs=whole(4),
        out_specs=whole(1)[0],
        out_shape=jax.ShapeDtypeStruct((columns, cells), F32),
        scratch_shapes=[VMEM((2 * columns, cells), BF)],
        compiler_params=params(24),
        name="own",
    )(x, a_hi, a_lo, diag)


def rim_update(part_ref, low_ref, high_ref, hi_ref, lo_ref, c):
    columns, cells = part_ref.shape
    lo_hi, lo_lo = split(low_ref[...])
    hi_hi, hi_lo = split(high_ref[...])
    top = jnp.concatenate([lo_hi, hi_hi], axis=1)
    rest = jnp.concatenate([lo_lo, hi_lo], axis=1)
    lanes = pl.ds(c * 256, 256)
    rows = pl.ds(cells, 2 * RIM)
    both = dot(jnp.concatenate([top, rest], axis=0), hi_ref[rows, lanes])
    return part_ref[:, lanes] + (both[0:columns] + both[columns:] + dot(top, lo_ref[rows, lanes]))


def rim_kernel(part_ref, low_ref, high_ref, hi_ref, lo_ref, out_ref, first_ref, last_ref):
    count = out_ref.shape[1] // 256
    for c in range(count):
        out = rim_update(part_ref, low_ref, high_ref, hi_ref, lo_ref, c)
        out_ref[:, c * 256 : (c + 1) * 256] = out
        if c == 0:
            first_ref[...] = out[:, 0:RIM]
        if c == count - 1:
            last_ref[...] = out[:, 256 - RIM :]


def rim(part, low, high, a_hi, a_lo):
    columns, cells = part.shape
    return pl.pallas_call(
        rim_kernel,
        in_specs=whole(5),
        out_specs=whole(3),
        out_shape=[
            jax.ShapeDtypeStruct((columns, cells), F32),
            jax.ShapeDtypeStruct((columns, RIM), F32),
            jax.ShapeDtypeStruct((columns, RIM), F32),
        ],
        compiler_params=params(24),
        name="rim",
    )(part, low, high, a_hi, a_lo)


def finish_kernel(
    part_ref, low_ref, high_ref, hi_ref, lo_ref, remapped_ref, rate_ref, mix_ref,
    out_ref, copy_ref,
):
    fields, levels = mix_ref.shape[0], mix_ref.shape[1]
    copy_ref[...] = remapped_ref[...]
    row = lax.broadcasted_iota(jnp.int32, (levels, 256), 0)
    mixes = [split(mix_ref[f]) for f in range(fields)]
    for c in range(part_ref.shape[1] // 256):
        mixed = rim_update(part_ref, low_ref, high_ref, hi_ref, lo_ref, c)
        at = pl.ds(c * 256, 256)
        for f in range(fields):
            mine = mixed[f * levels : (f + 1) * levels]
            top = mine[0:1]
            top = top + rate_ref[f : f + 1, at] * (remapped_ref[f : f + 1, at] - top)
            forced = jnp.where(row == 0, jnp.broadcast_to(top, mine.shape), mine)
            hi, lo = split(forced)
            m_hi, m_lo = mixes[f]
            out_ref[f, :, at] = dot(m_hi, hi) + (dot(m_hi, lo) + dot(m_lo, hi))


def finish(part, low, high, a_hi, a_lo, remapped, rate, mix):
    columns, cells = part.shape
    fields, levels = mix.shape[0], mix.shape[1]
    return pl.pallas_call(
        finish_kernel,
        in_specs=whole(8),
        out_specs=whole(2),
        out_shape=[
            jax.ShapeDtypeStruct((fields, levels, cells), F32),
            jax.ShapeDtypeStruct((fields, cells), F32),
        ],
        compiler_params=params(24),
        name="finish",
    )(part, low, high, a_hi, a_lo, remapped, rate, mix)


def row16(row):
    return jnp.broadcast_to(row, (16, LANE))


def pack_kernel(
    state_ref, source_ref, owner_ref, cell_ref, weight_ref, out_ref,
    tiles_ref, slot_ref, owner_f_ref, piece_ref, hot_ref, rank_ref, left_ref, right_ref, acc_ref,
):
    fields = state_ref.shape[0]
    rows = source_ref.shape[0]
    blocks = out_ref.shape[0] // 16
    chunk = right_ref.shape[1]
    per = chunk // LANE
    groups = blocks // 2
    owner_f_ref[...] = owner_ref[...].astype(F32)
    cell = cell_ref[...]
    piece_ref[0:rows, :] = ((cell // 16) * 16).astype(F32)
    piece_ref[rows:, :] = (cell % 16).astype(F32)
    source = source_ref[...]
    line, lane = source // LANE, source % LANE
    for f in range(fields):
        got = jnp.zeros((rows, LANE), F32)
        for h in range(state_ref.shape[2] // LANE):
            table = jnp.broadcast_to(state_ref[f, 0:1, h * LANE : (h + 1) * LANE], (rows, LANE))
            one = jnp.take_along_axis(table, lane, axis=1, mode="promise_in_bounds")
            got = jnp.where(line == h, one, got)
        got = got * weight_ref[...]
        hi = got.astype(BF).astype(F32)
        tiles_ref[pl.ds(f, rows, stride=2 * fields), :] = hi
        tiles_ref[pl.ds(fields + f, rows, stride=2 * fields), :] = got - hi
    i16 = lax.broadcasted_iota(jnp.int32, (16, LANE), 0).astype(F32)
    i0 = lax.broadcasted_iota(jnp.int32, (LANE, 2 * LANE), 0)
    i1 = lax.broadcasted_iota(jnp.int32, (LANE, 2 * LANE), 1)
    before = jnp.where(i0 < i1, 1.0, 0.0).astype(BF)
    one16 = jnp.ones((16, LANE), BF)
    zero16 = jnp.zeros((16, LANE), BF)
    for r in range(rows):
        who = row16(owner_f_ref[r : r + 1, :]).astype(BF)
        for j in range(blocks // 16):
            here = (i16 + j * 16).astype(BF) == who
            hot_ref[r * blocks + j * 16 : r * blocks + (j + 1) * 16, :] = jnp.where(here, one16, zero16)
    rank_ref[...] = dot(hot_ref[...], before)
    base = jnp.zeros((blocks, LANE), F32)
    for r in range(rows):
        at = pl.ds(r * blocks, blocks)
        hot = hot_ref[at, :].astype(F32)
        slot_ref[r : r + 1, :] = jnp.sum(hot * (rank_ref[at, 0:LANE] + base), axis=0, keepdims=True)
        base = base + rank_ref[at, LANE:]

    acc_ref[...] = jnp.zeros_like(acc_ref)
    eight = jnp.where(i16 < 8, 0.0, 1.0)

    def body(c, _):
        for t in range(per):
            r = c * per + t
            at = pl.ds(t * LANE, LANE)
            one = pl.ds(r, 1)
            tile = tiles_ref[pl.ds(pl.multiple_of(r * 8, 8), 8), :]
            tile = jnp.concatenate([tile, tile], axis=0).astype(BF)
            owner = row16(owner_f_ref[one, :])
            who = (owner - eight).astype(BF)
            for o in range(groups):
                left_ref[o * 16 : (o + 1) * 16, at] = jnp.where(who == 2 * o, tile, zero16)
            who = (owner - i16).astype(BF)
            for part in range(2):
                piece = row16(piece_ref[pl.ds(part * rows + r, 1), :]).astype(BF)
                for o in range(blocks // 16):
                    top = groups * 16 + part * blocks + o * 16
                    left_ref[top : top + 16, at] = jnp.where(who == 16 * o, piece, zero16)
            who = row16(slot_ref[one, :]).astype(BF)
            for o in range(2 * LANE // 16):
                here = (i16 + o * 16).astype(BF) == who
                right_ref[o * 16 : (o + 1) * 16, at] = jnp.where(here, one16, zero16)
        acc_ref[...] += dot_nt(left_ref[...], right_ref[...])
        return 0

    lax.fori_loop(0, rows // per, body, 0)
    low = lax.broadcasted_iota(jnp.int32, (8, LANE), 0) < 4
    for o in range(blocks):
        at = pl.ds(o * 8, 8)
        left, right = acc_ref[at, 0:LANE], acc_ref[at, LANE:]
        left = left + pltpu.roll(left, 4, 0)
        right = right + pltpu.roll(right, 4, 0)
        out_ref[o * 16 : o * 16 + 8, :] = jnp.where(low, left, right)
    top = blocks * 8
    for h in range(2):
        lanes = pl.ds(h * LANE, LANE)
        out_ref[pl.ds(8 + h, blocks, stride=16), :] = (
            acc_ref[top : top + blocks, lanes] + acc_ref[top + blocks :, lanes]
        )


def pack(state, source, owner, cell, weight, blocks):
    fields, levels, cells = state.shape
    rows = source.shape[0]
    chunk = 512
    return pl.pallas_call(
        pack_kernel,
        grid=(1,),
        in_specs=[pl.BlockSpec((fields, 8, cells), lambda i: (0, 0, 0))] + whole(4),
        out_specs=whole(1)[0],
        out_shape=jax.ShapeDtypeStruct((blocks * 16, LANE), F32),
        scratch_shapes=[
            VMEM((rows * 2 * fields, LANE), F32),
            VMEM((rows, LANE), F32),
            VMEM((rows, LANE), F32),
            VMEM((2 * rows, LANE), F32),
            VMEM((rows * blocks, LANE), BF),
            VMEM((rows * blocks, 2 * LANE), F32),
            VMEM((blocks * 10, chunk), BF),
            VMEM((2 * LANE, chunk), BF),
            VMEM((blocks * 10, 2 * LANE), F32),
        ],
        compiler_params=params(20),
        name="pack",
    )(state, source, owner, cell, weight)


def unpack_kernel(in_ref, out_ref, left_ref, right_ref):
    fields, cells = out_ref.shape
    blocks = in_ref.shape[0] // 16
    groups = cells // 256
    chunk = right_ref.shape[1]
    per = chunk // (2 * LANE)
    i16 = lax.broadcasted_iota(jnp.int32, (16, LANE), 0).astype(F32)
    eight = jnp.where(i16 < 8, 0.0, 1.0)
    one16 = jnp.ones((16, LANE), BF)
    zero16 = jnp.zeros((16, LANE), BF)

    def body(c, acc):
        for t in range(2 * per):
            top = pl.multiple_of((c * per + t // 2) * 16, 16)
            at = pl.ds(t * LANE, LANE)
            cell = in_ref[pl.ds(top + 8 + t % 2, 1), :].astype(jnp.int32)
            group = (cell // 256).astype(F32)
            local = row16((cell % 256).astype(F32)).astype(BF)
            vals = in_ref[pl.ds(top, 8), :][(t % 2) * 4 : (t % 2) * 4 + 4]
            hi = vals.astype(BF).astype(F32)
            lo = vals - hi
            tile = jnp.concatenate([hi, lo, hi, lo], axis=0).astype(BF)
            who = (row16(group) - eight).astype(BF)
            for g in range(groups // 2):
                left_ref[g * 16 : (g + 1) * 16, at] = jnp.where(who == 2 * g, tile, zero16)
            for o in range(16):
                here = (i16 + o * 16).astype(BF) == local
                right_ref[o * 16 : (o + 1) * 16, at] = jnp.where(here, one16, zero16)
        return acc + dot_nt(left_ref[...], right_ref[...])

    acc = lax.fori_loop(0, blocks // per, body, jnp.zeros((groups * 8, 256), F32))
    for g in range(groups):
        out_ref[:, g * 256 : (g + 1) * 256] = acc[g * 8 : g * 8 + 4] + acc[g * 8 + 4 : g * 8 + 8]


def unpack(packed, fields, count):
    chunk = 1024
    return pl.pallas_call(
        unpack_kernel,
        in_specs=whole(1),
        out_specs=whole(1)[0],
        out_shape=jax.ShapeDtypeStruct((fields, count), F32),
        scratch_shapes=[VMEM((count // 256 * 8, chunk), BF), VMEM((256, chunk), BF)],
        compiler_params=params(16),
        name="unpack",
    )(packed)


def per_device(
    state, neighbour, edge_weight, coupling_rate, vertical_mix,
    remap_source, remap_owner, remap_cell, remap_weight,
):
    fields, levels, cells = state.shape[1:]
    columns = fields * levels
    blocks = lax.axis_size("blk")
    forward = [(i, (i + 1) % blocks) for i in range(blocks)]
    backward = [(b, a) for a, b in forward]

    def lines(x):
        return x.reshape(-1, LANE)

    def exchange(first, last):
        low = lax.ppermute(last, "blk", forward)
        high = lax.ppermute(first, "blk", backward)
        return low, high

    x = state.reshape(columns, cells)
    halo = exchange(x[:, :RIM], x[:, cells - RIM :])
    packed = pack(
        state[0], lines(remap_source), lines(remap_owner), lines(remap_cell),
        lines(remap_weight), blocks,
    )
    packed = lax.all_to_all(packed.reshape(blocks, 16, LANE), "blk", 0, 0, tiled=True)
    a_hi, a_lo, diag = build(lines(neighbour), lines(edge_weight), cells)
    for step in range(SUB - 1):
        part = own(x, a_hi, a_lo, diag)
        x, first, last = rim(part, *halo, a_hi, a_lo)
        halo = exchange(first, last)
    part = own(x, a_hi, a_lo, diag)
    partial_sum = unpack(packed.reshape(blocks * 16, LANE), fields, cells)
    remapped = lax.ppermute(partial_sum, "sec", [(0, 1), (1, 0)])
    out, remapped = finish(part, *halo, a_hi, a_lo, remapped, coupling_rate[0], vertical_mix[0])
    return out[None], remapped[None]


def solution(mesh):
    return jax.shard_map(
        per_device,
        mesh=mesh,
        in_specs=(
            P("sec", None, None, "blk"),
            P("sec", None, "blk"),
            P("sec", None, "blk"),
            P("sec", None, "blk"),
            P("sec", None, None, None),
            P("sec", "blk"),
            P("sec", "blk", None),
            P("sec", "blk"),
            P("sec", "blk"),
        ),
        out_specs=(P("sec", None, None, "blk"), P("sec", None, "blk")),
        check_vma=False,
    )
```

time: 794 us -> 97.6 us (0.12)
  the two profiles are of different devices: /device:TPU:65 before, /device:TPU:1 now
where the time goes in v2:
time: 97.6 us; the launch traced here: 96.8 us
  starting transfers between devices  42.9 us (44%)
  Pallas kernels  37.8 us (39%)
  local copies, waits for them, and re-layouts  15.3 us (16%)
    ppermute x4, starting transfers between devices, exchange(): high = lax.ppermute(first, 'blk', backward)  27.5 us
    unnamed x28, local copies, waits for them, and re-layouts  14.5 us
    all_to_all x1, starting transfers between devices, per_device(): lax.all_to_all(packed.reshape(blocks, 16, LANE), 'blk', 0, 0, tiled=True)  12 us
    pallas_call x4, Pallas kernels, own(): pl.pallas_call(own_kernel, in_specs=whole(4), out_specs=whole(1)[0], out_...  11 us
    pallas_call x1, Pallas kernels, pack(): pl.pallas_call(pack_kernel, grid=(1,), in_specs=[pl.BlockSpec((fields, 8,...  8.98 us
    pallas_call x1, Pallas kernels, build(): pl.pallas_call(build_kernel, in_specs=whole(2), out_specs=whole(3), out_s...  8.05 us
    pallas_call x1, Pallas kernels, unpack(): pl.pallas_call(unpack_kernel, in_specs=whole(1), out_specs=whole(1)[0], o...  5.53 us
    ppermute x1, starting transfers between devices, per_device(): remapped = lax.ppermute(partial_sum, 'sec', [(0, 1), (1, 0)])  3.25 us
  transfers between devices with their start and end apart: 10, of which 0 were waited for; matrix products, arithmetic and copies ran while one was open for 1% of the time, Pallas kernels for 27%

profile of v2, /device:TPU:1, one launch (start us, length us, event | category | flops | bytes accessed | tf_op | source)
XLA Modules:
  0.0 96.8 jit_solution(12019532890038169814)
XLA Ops:
  0.6 1.0 %copy-done.4 = f32[1,4,16,2048]{3,2,1,0:T(8,128)S(1)} copy-done((f32[1,4,16,2048]{3,2,1,0:T(8,128)S(1)}, f32[1,4,16,2048]{3,2,1,0:T(8,128)}, u32[]{:S(2)}) %copy-start.4) | copy-done | bytes 524312
  1.7 0.8 copy-done.10
  2.4 0.8 copy-done.11
  3.2 0.8 copy-done.12
  4.7 9.0 %pack.1 = f32[1024,128]{1,0:T(8,128)} custom-call(f32[4,16,2048]{2,1,0:T(8,128)S(1)} %bitcast.15, s32[64,128]{1,0:T(8,128)S(1)} %bitcast.22, s32[64,128]{1,0:T(8,128)S(1)} %bitcast.23, s32[64,128]{1,0:T(8,128)S(1)} %bitcast.24, f32[64,128]{1,0:T(8,128)S(1)} %bitcast.25), custom_call_target="tpu_custom_call" | custom-call | tf_op jit(solution)/shard_map/pack/pallas_call | solution.py:302
  13.7 12.0 %all-to-all-start = ((f32[64,16,128]{2,1,0:T(8,128)}), f32[64,16,128]{2,1,0:T(8,128)S(1)}, u32[]{:S(2)}, u32[]{:S(2)}) async-start(f32[64,16,128]{2,1,0:T(8,128)} %bitcast.8), calls=%async_computation | async-start | bytes 1048576 | tf_op jit(solution)/shard_map/all_to_all | solution.py:396
  25.7 0.8 fusion
  26.4 6.8 %collective-permute-start.1 = (f32[64,128]{1,0:T(8,128)S(1)}, f32[64,128]{1,0:T(8,128)S(1)}, u32[]{:S(2)}, u32[]{:S(2)}) collective-permute-start(f32[64,128]{1,0:T(8,128)S(1)} %get-tuple-element.30), channel_id=1, source_target_pairs={{1,0},{2,1},{3,2},{4,3},{5,4},{6,5},{7,6},{8,7},{9,8},{10,9},{11,1... | collective-permute-start | bytes 98312 | tf_op jit(solution)/shard_map/ppermute | solution.py:387
  33.2 0.8 copy-done.6
  34.0 0.8 copy-done.7
  34.8 8.1 %build.1 = (bf16[2304,2048]{1,0:T(8,128)(2,1)S(1)}, bf16[2304,2048]{1,0:T(8,128)(2,1)S(1)}, f32[1,2048]{1,0:T(1,128)S(1)}) custom-call(s32[96,128]{1,0:T(8,128)S(1)} %bitcast.18, f32[96,128]{1,0:T(8,128)S(1)} %bitcast.19), custom_call_target="tpu_custom_call" | custom-call | tf_op jit(solution)/shard_map/build/pallas_call | solution.py:91
  42.9 1.4 %copy-done.5 = f32[1,4,16,2048]{3,2,1,0:T(8,128)S(1)} copy-done((f32[1,4,16,2048]{3,2,1,0:T(8,128)S(1)}, f32[1,4,16,2048]{3,2,1,0:T(8,128)}, u32[]{:S(2)}) %copy-start.5) | copy-done | bytes 524312
  44.3 2.7 %own.4.part_ref = f32[64,2048]{1,0:T(8,128)S(1)} custom-call(f32[64,2048]{1,0:T(8,128)S(1)} %bitcast.16, bf16[2304,2048]{1,0:T(8,128)(2,1)S(1)} %get-tuple-element.16.hi_ref, bf16[2304,2048]{1,0:T(8,128)(2,1)S(1)} %get-tuple-element.17.lo_ref, f32[1,2048]{1,0:T(1,128)S(1)} %get-tuple-element.18.diag_ref), custom_call_target="tpu_custom_call" | custom-call | tf_op jit(solution)/shard_map/own/pallas_call | solution.py:119
  47.6 7.0 %collective-permute-start.3 = (f32[64,128]{1,0:T(8,128)S(1)}, f32[64,128]{1,0:T(8,128)S(1)}, u32[]{:S(2)}, u32[]{:S(2)}) collective-permute-start(f32[64,128]{1,0:T(8,128)S(1)} %get-tuple-element.21), channel_id=1, source_target_pairs={{1,0},{2,1},{3,2},{4,3},{5,4},{6,5},{7,6},{8,7},{9,8},{10,9},{11,1... | collective-permute-start | bytes 98312 | tf_op jit(solution)/shard_map/ppermute | solution.py:387
  54.6 2.7 %own.5.part_ref = f32[64,2048]{1,0:T(8,128)S(1)} custom-call(f32[64,2048]{1,0:T(8,128)S(1)} %get-tuple-element.19.x_ref, bf16[2304,2048]{1,0:T(8,128)(2,1)S(1)} %get-tuple-element.16.hi_ref, bf16[2304,2048]{1,0:T(8,128)(2,1)S(1)} %get-tuple-element.17.lo_ref, f32[1,2048]{1,0:T(1,128)S(1)} %get-tuple-element.18.diag_ref), custom_call_target="tpu_custom_call" | custom-call | tf_op jit(solution)/shard_map/own/pallas_call | solution.py:119
  57.9 6.9 %collective-permute-start.5 = (f32[64,128]{1,0:T(8,128)S(1)}, f32[64,128]{1,0:T(8,128)S(1)}, u32[]{:S(2)}, u32[]{:S(2)}) collective-permute-start(f32[64,128]{1,0:T(8,128)S(1)} %get-tuple-element.24), channel_id=1, source_target_pairs={{1,0},{2,1},{3,2},{4,3},{5,4},{6,5},{7,6},{8,7},{9,8},{10,9},{11,1... | collective-permute-start | bytes 98312 | tf_op jit(solution)/shard_map/ppermute | solution.py:387
  64.8 2.7 %own.6.part_ref = f32[64,2048]{1,0:T(8,128)S(1)} custom-call(f32[64,2048]{1,0:T(8,128)S(1)} %get-tuple-element.22.x_ref, bf16[2304,2048]{1,0:T(8,128)(2,1)S(1)} %get-tuple-element.16.hi_ref, bf16[2304,2048]{1,0:T(8,128)(2,1)S(1)} %get-tuple-element.17.lo_ref, f32[1,2048]{1,0:T(1,128)S(1)} %get-tuple-element.18.diag_ref), custom_call_target="tpu_custom_call" | custom-call | tf_op jit(solution)/shard_map/own/pallas_call | solution.py:119
  68.2 6.9 %collective-permute-start.7 = (f32[64,128]{1,0:T(8,128)S(1)}, f32[64,128]{1,0:T(8,128)S(1)}, u32[]{:S(2)}, u32[]{:S(2)}) collective-permute-start(f32[64,128]{1,0:T(8,128)S(1)} %get-tuple-element.27), channel_id=1, source_target_pairs={{1,0},{2,1},{3,2},{4,3},{5,4},{6,5},{7,6},{8,7},{9,8},{10,9},{11,1... | collective-permute-start | bytes 98312 | tf_op jit(solution)/shard_map/ppermute | solution.py:387
  75.1 5.5 %unpack.1 = f32[4,2048]{1,0:T(4,128)S(1)} custom-call(f32[1024,128]{1,0:T(8,128)S(1)} %bitcast.17), custom_call_target="tpu_custom_call" | custom-call | tf_op jit(solution)/shard_map/unpack/pallas_call | solution.py:361
  80.6 3.3 %collective-permute-start.8 = (f32[4,2048]{1,0:T(4,128)S(1)}, f32[4,2048]{1,0:T(4,128)S(1)}, u32[]{:S(2)}, u32[]{:S(2)}) collective-permute-start(f32[4,2048]{1,0:T(4,128)S(1)} %unpack.1), channel_id=1, source_target_pairs={{0,64},{64,0},{1,65},{65,1},{2,66},{66,2},{3,67},{67,3},{4,68},{68... | collective-permute-start | bytes 98312 | tf_op jit(solution)/shard_map/ppermute | solution.py:404
  83.9 3.7 %copy-done.1 = bf16[2304,2048]{1,0:T(8,128)(2,1)S(1)} copy-done((bf16[2304,2048]{1,0:T(8,128)(2,1)S(1)}, bf16[2304,2048]{1,0:T(8,128)(2,1)}, u32[]{:S(2)}) %copy-start.1) | copy-done | bytes 9437208
  87.5 3.7 %copy-done.3 = bf16[2304,2048]{1,0:T(8,128)(2,1)S(1)} copy-done((bf16[2304,2048]{1,0:T(8,128)(2,1)S(1)}, bf16[2304,2048]{1,0:T(8,128)(2,1)}, u32[]{:S(2)}) %copy-start.3) | copy-done | bytes 9437208
  91.2 2.7 %own.7.part_ref = f32[64,2048]{1,0:T(8,128)S(1)} custom-call(f32[64,2048]{1,0:T(8,128)S(1)} %get-tuple-element.25.x_ref, bf16[2304,2048]{1,0:T(8,128)(2,1)S(1)} %copy-done.1, bf16[2304,2048]{1,0:T(8,128)(2,1)S(1)} %copy-done.3, f32[1,2048]{1,0:T(1,128)S(1)} %get-tuple-element.18.diag_ref), custom_call_target="tpu_custom_call" | custom-call | tf_op jit(solution)/shard_map/own/pallas_call | solution.py:119
  94.0 2.8 %finish.1 = (f32[4,16,2048]{2,1,0:T(8,128)}, f32[4,2048]{1,0:T(4,128)}) custom-call(f32[64,2048]{1,0:T(8,128)S(1)} %own.7.part_ref, f32[64,128]{1,0:T(8,128)S(1)} %collective-permute-done.6.low_ref, f32[64,128]{1,0:T(8,128)S(1)} %collective-permute-done.7.high_ref, bf16[2304,2048]{1,0:T(8,128)(2,1)S(1)} %copy-done.1, bf16[2304,2048]{1,0:T(8,128)(2,1)S(1)} %copy-done.3, ...), custom_call_target="tpu_custom_call" | custom-call | tf_op jit(solution)/shard_map/finish/pallas_call | solution.py:193
  (36 shorter events, 2.5 us)
Async XLA Ops:
  0.6 1.0 %copy-start.4 = (f32[1,4,16,2048]{3,2,1,0:T(8,128)S(1)}, f32[1,4,16,2048]{3,2,1,0:T(8,128)}, u32[]{:S(2)}) copy-start(f32[1,4,16,2048]{3,2,1,0:T(8,128)} %param.9) | copy-start | bytes 1572868
  1.7 0.8 copy-start.10
  2.4 0.8 copy-start.11
  3.2 0.8 copy-start.12
  4.0 0.8 copy-start.13
  13.7 61.4 %all-to-all-start = ((f32[64,16,128]{2,1,0:T(8,128)}), f32[64,16,128]{2,1,0:T(8,128)S(1)}, u32[]{:S(2)}, u32[]{:S(2)}) async-start(f32[64,16,128]{2,1,0:T(8,128)} %bitcast.8), calls=%async_computation | async-start | bytes 1048576 | tf_op jit(solution)/shard_map/all_to_all | solution.py:396
  26.4 20.6 %collective-permute-start.1 = (f32[64,128]{1,0:T(8,128)S(1)}, f32[64,128]{1,0:T(8,128)S(1)}, u32[]{:S(2)}, u32[]{:S(2)}) collective-permute-start(f32[64,128]{1,0:T(8,128)S(1)} %get-tuple-element.30), channel_id=1, source_target_pairs={{1,0},{2,1},{3,2},{4,3},{5,4},{6,5},{7,6},{8,7},{9,8},{10,9},{11,1... | collective-permute-start | bytes 98312 | tf_op jit(solution)/shard_map/ppermute | solution.py:387
  33.2 13.9 %collective-permute-start = (f32[64,128]{1,0:T(8,128)S(1)}, f32[64,128]{1,0:T(8,128)S(1)}, u32[]{:S(2)}, u32[]{:S(2)}) collective-permute-start(f32[64,128]{1,0:T(8,128)S(1)} %get-tuple-element.31), channel_id=1, source_target_pairs={{0,1},{1,2},{2,3},{3,4},{4,5},{5,6},{6,7},{7,8},{8,9},{9,10},{10,1... | collective-permute-start | bytes 98312 | tf_op jit(solution)/shard_map/ppermute | solution.py:386
  33.2 0.8 copy-start.6
  34.0 0.8 copy-start.7
  42.8 24.7 %copy-start = (bf16[2304,2048]{1,0:T(8,128)(2,1)}, bf16[2304,2048]{1,0:T(8,128)(2,1)S(1)}, u32[]{:S(2)}) copy-start(bf16[2304,2048]{1,0:T(8,128)(2,1)S(1)} %get-tuple-element.16.hi_ref) | copy-start | bytes 28311556
  42.9 24.7 %copy-start.2 = (bf16[2304,2048]{1,0:T(8,128)(2,1)}, bf16[2304,2048]{1,0:T(8,128)(2,1)S(1)}, u32[]{:S(2)}) copy-start(bf16[2304,2048]{1,0:T(8,128)(2,1)S(1)} %get-tuple-element.17.lo_ref) | copy-start | bytes 28311556
  42.9 1.4 %copy-start.5 = (f32[1,4,16,2048]{3,2,1,0:T(8,128)S(1)}, f32[1,4,16,2048]{3,2,1,0:T(8,128)}, u32[]{:S(2)}) copy-start(f32[1,4,16,2048]{3,2,1,0:T(8,128)} %param.9) | copy-start | bytes 1572868
  47.6 9.8 %collective-permute-start.2 = (f32[64,128]{1,0:T(8,128)S(1)}, f32[64,128]{1,0:T(8,128)S(1)}, u32[]{:S(2)}, u32[]{:S(2)}) collective-permute-start(f32[64,128]{1,0:T(8,128)S(1)} %get-tuple-element.20), channel_id=1, source_target_pairs={{0,1},{1,2},{2,3},{3,4},{4,5},{5,6},{6,7},{7,8},{8,9},{9,10},{10,1... | collective-permute-start | bytes 98312 | tf_op jit(solution)/shard_map/ppermute | solution.py:386
  47.6 9.7 %collective-permute-start.3 = (f32[64,128]{1,0:T(8,128)S(1)}, f32[64,128]{1,0:T(8,128)S(1)}, u32[]{:S(2)}, u32[]{:S(2)}) collective-permute-start(f32[64,128]{1,0:T(8,128)S(1)} %get-tuple-element.21), channel_id=1, source_target_pairs={{1,0},{2,1},{3,2},{4,3},{5,4},{6,5},{7,6},{8,7},{9,8},{10,9},{11,1... | collective-permute-start | bytes 98312 | tf_op jit(solution)/shard_map/ppermute | solution.py:387
  57.9 9.7 %collective-permute-start.4 = (f32[64,128]{1,0:T(8,128)S(1)}, f32[64,128]{1,0:T(8,128)S(1)}, u32[]{:S(2)}, u32[]{:S(2)}) collective-permute-start(f32[64,128]{1,0:T(8,128)S(1)} %get-tuple-element.23), channel_id=1, source_target_pairs={{0,1},{1,2},{2,3},{3,4},{4,5},{5,6},{6,7},{7,8},{8,9},{9,10},{10,1... | collective-permute-start | bytes 98312 | tf_op jit(solution)/shard_map/ppermute | solution.py:386
  57.9 9.6 %collective-permute-start.5 = (f32[64,128]{1,0:T(8,128)S(1)}, f32[64,128]{1,0:T(8,128)S(1)}, u32[]{:S(2)}, u32[]{:S(2)}) collective-permute-start(f32[64,128]{1,0:T(8,128)S(1)} %get-tuple-element.24), channel_id=1, source_target_pairs={{1,0},{2,1},{3,2},{4,3},{5,4},{6,5},{7,6},{8,7},{9,8},{10,9},{11,1... | collective-permute-start | bytes 98312 | tf_op jit(solution)/shard_map/ppermute | solution.py:387
  68.1 25.9 %collective-permute-start.6 = (f32[64,128]{1,0:T(8,128)S(1)}, f32[64,128]{1,0:T(8,128)S(1)}, u32[]{:S(2)}, u32[]{:S(2)}) collective-permute-start(f32[64,128]{1,0:T(8,128)S(1)} %get-tuple-element.26), channel_id=1, source_target_pairs={{0,1},{1,2},{2,3},{3,4},{4,5},{5,6},{6,7},{7,8},{8,9},{9,10},{10,1... | collective-permute-start | bytes 98312 | tf_op jit(solution)/shard_map/ppermute | solution.py:386
  68.2 25.8 %collective-permute-start.7 = (f32[64,128]{1,0:T(8,128)S(1)}, f32[64,128]{1,0:T(8,128)S(1)}, u32[]{:S(2)}, u32[]{:S(2)}) collective-permute-start(f32[64,128]{1,0:T(8,128)S(1)} %get-tuple-element.27), channel_id=1, source_target_pairs={{1,0},{2,1},{3,2},{4,3},{5,4},{6,5},{7,6},{8,7},{9,8},{10,9},{11,1... | collective-permute-start | bytes 98312 | tf_op jit(solution)/shard_map/ppermute | solution.py:387
  80.6 13.4 %collective-permute-start.8 = (f32[4,2048]{1,0:T(4,128)S(1)}, f32[4,2048]{1,0:T(4,128)S(1)}, u32[]{:S(2)}, u32[]{:S(2)}) collective-permute-start(f32[4,2048]{1,0:T(4,128)S(1)} %unpack.1), channel_id=1, source_target_pairs={{0,64},{64,0},{1,65},{65,1},{2,66},{66,2},{3,67},{67,3},{4,68},{68... | collective-permute-start | bytes 98312 | tf_op jit(solution)/shard_map/ppermute | solution.py:404
  83.9 3.7 %copy-start.1 = (bf16[2304,2048]{1,0:T(8,128)(2,1)S(1)}, bf16[2304,2048]{1,0:T(8,128)(2,1)}, u32[]{:S(2)}) copy-start(bf16[2304,2048]{1,0:T(8,128)(2,1)} %copy-done) | copy-start | bytes 28311556
  87.5 3.7 %copy-start.3 = (bf16[2304,2048]{1,0:T(8,128)(2,1)S(1)}, bf16[2304,2048]{1,0:T(8,128)(2,1)}, u32[]{:S(2)}) copy-start(bf16[2304,2048]{1,0:T(8,128)(2,1)} %copy-done.2) | copy-start | bytes 28311556
  91.2 2.8 %copy-start.8 = (f32[1,4,2048]{2,1,0:T(4,128)S(1)}, f32[1,4,2048]{2,1,0:T(4,128)}, u32[]{:S(2)}) copy-start(f32[1,4,2048]{2,1,0:T(4,128)} %param.12) | copy-start | bytes 98308
  91.2 2.8 %copy-start.9 = (f32[1,4,16,16]{3,2,1,0:T(8,128)S(1)}, f32[1,4,16,16]{3,2,1,0:T(8,128)}, u32[]{:S(2)}) copy-start(f32[1,4,16,16]{3,2,1,0:T(8,128)} %param.13) | copy-start | bytes 12292

commit v3 on v2

--- a/solution.py
+++ b/solution.py
@@ -27,55 +27,145 @@
     return hi, lo
 
 
-def build_kernel(nbr_ref, w_ref, hi_ref, lo_ref, diag_ref):
-    rows, cells = hi_ref.shape
+def build_tile(nbr_ref, w_ref, hi_ref, lo_ref, diag_ref, i, to):
+    rows = hi_ref.shape[0]
+    cells = rows - 2 * RIM
     lines = cells // LANE
     slots = nbr_ref.shape[0] // lines
     step = 16
     first = lax.broadcasted_iota(jnp.int32, (step, LANE), 0).astype(F32)
+    lanes = pl.ds(to * LANE if isinstance(to, int) else pl.multiple_of(to * LANE, LANE), LANE)
+    pos, wgt = [], []
+    for k in range(slots):
+        p = nbr_ref[pl.ds(k * lines + i, 1), :]
+        p = jnp.where(p < RIM, p + cells, jnp.where(p < cells + RIM, p - RIM, p))
+        pos.append(p)
+        wgt.append(w_ref[pl.ds(k * lines + i, 1), :])
+    total = wgt[0]
+    for k in range(1, slots):
+        total = total + wgt[k]
+    diag_ref[:, lanes] = 1.0 - total
+    for k in range(1, slots):
+        for j in range(k):
+            same = pos[j] == pos[k]
+            wgt[j] = jnp.where(same, wgt[j] + wgt[k], wgt[j])
+            pos[k] = jnp.where(same, -1, pos[k])
+    whi, wlo = [], []
+    for k in range(slots):
+        hi = wgt[k].astype(BF).astype(F32)
+        whi.append(jnp.broadcast_to(hi, (step, LANE)).astype(BF))
+        wlo.append(jnp.broadcast_to(wgt[k] - hi, (step, LANE)).astype(BF))
+    for block in range(rows // 256):
+        loc = []
+        for k in range(slots):
+            local = pos[k] - block * 256
+            local = jnp.where((local >= 0) & (local < 256), local, -1).astype(F32)
+            loc.append(jnp.broadcast_to(local, (step, LANE)).astype(BF))
+        for part in range(256 // step):
+            row = (first + part * step).astype(BF)
+            hi = jnp.zeros((step, LANE), BF)
+            lo = jnp.zeros((step, LANE), BF)
+            for k in range(slots):
+                here = row == loc[k]
+                hi = jnp.where(here, whi[k], hi)
+                lo = jnp.where(here, wlo[k], lo)
+            at = pl.ds(block * 256 + part * step, step)
+            hi_ref[at, lanes] = hi
+            lo_ref[at, lanes] = lo
+
+
+def fetch(pairs, sems):
+    copies = [pltpu.make_async_copy(a, b, sems.at[n]) for n, (a, b) in enumerate(pairs)]
+    for copy in copies:
+        copy.start()
+    return copies
+
+
+def odd_block():
+    return lax.axis_index("blk") % 2 == 1
+
+
+def sides(pair_ref, other_ref):
+    odd = odd_block()
+    pair, other = pair_ref[...], other_ref[...]
+    return jnp.where(odd, pair, other), jnp.where(odd, other, pair)
+
+
+def send(first, last, pair_ref, other_ref):
+    odd = odd_block()
+    pair_ref[...] = jnp.where(odd, first, last)
+    other_ref[...] = jnp.where(odd, last, first)
+
+
+def fill_cat(cat_ref, x_ref, pair_ref, other_ref):
+    columns, cells = x_ref.shape
+    low, high = sides(pair_ref, other_ref)
+    for value, at in (
+        (x_ref[...], pl.ds(0, cells)),
+        (low, pl.ds(cells, RIM)),
+        (high, pl.ds(cells + RIM, RIM)),
+    ):
+        hi, lo = split(value)
+        cat_ref[0:columns, at] = hi
+        cat_ref[columns:, at] = lo
+
+
+def product(cat_ref, hi_ref, lo_ref, rows, lanes):
+    columns = cat_ref.shape[0] // 2
+    at = pl.ds(0, rows)
+    both = dot(cat_ref[:, at], hi_ref[at, lanes])
+    low = dot(cat_ref[0:columns, at], lo_ref[at, lanes])
+    return both[0:columns] + both[columns:] + low
+
+
+def edge_kernel(
+    nbr_hbm, w_hbm, x_hbm, pair_ref, other_ref, pair_out, other_out,
+    nbr_ref, w_ref, x_ref, hi_ref, lo_ref, diag_ref, cat_ref, sems,
+):
+    copies = fetch(((nbr_hbm, nbr_ref), (w_hbm, w_ref), (x_hbm, x_ref)), sems)
+    rows, cells = hi_ref.shape[0], x_ref.shape[1]
+    copies[0].wait()
+    copies[1].wait()
+    last = cells // LANE - 1
+    build_tile(nbr_ref, w_ref, hi_ref, lo_ref, diag_ref, 0, 0)
+    build_tile(nbr_ref, w_ref, hi_ref, lo_ref, diag_ref, last, 1)
+    copies[2].wait()
+    fill_cat(cat_ref, x_ref, pair_ref, other_ref)
+    ends = []
+    for n, i in enumerate((0, last)):
+        lanes, mine = pl.ds(i * LANE, LANE), pl.ds(n * LANE, LANE)
+        ends.append(
+            diag_ref[:, mine] * x_ref[:, lanes] + product(cat_ref, hi_ref, lo_ref, rows, mine)
+        )
+    send(*ends, pair_out, other_out)
+
+
+def main_kernel(
+    nbr_hbm, w_hbm, x_hbm, pair_ref, other_ref,
+    hi_ref, lo_ref, diag_ref, out_ref, nbr_ref, w_ref, x_ref, cat_ref, y_ref, sems,
+):
+    copies = fetch(((nbr_hbm, nbr_ref), (w_hbm, w_ref), (x_hbm, x_ref)), sems)
+    rows, cells = hi_ref.shape
+    columns = x_ref.shape[0]
+    copies[0].wait()
+    copies[1].wait()
 
     def body(i, _):
-        lanes = pl.ds(pl.multiple_of(i * LANE, LANE), LANE)
-        pos, wgt = [], []
-        for k in range(slots):
-            p = nbr_ref[pl.ds(k * lines + i, 1), :]
-            p = jnp.where(p < RIM, p + cells, jnp.where(p < cells + RIM, p - RIM, p))
-            pos.append(p)
-            wgt.append(w_ref[pl.ds(k * lines + i, 1), :])
-        total = wgt[0]
-        for k in range(1, slots):
-            total = total + wgt[k]
-        diag_ref[:, lanes] = 1.0 - total
-        for k in range(1, slots):
-            for j in range(k):
-                same = pos[j] == pos[k]
-                wgt[j] = jnp.where(same, wgt[j] + wgt[k], wgt[j])
-                pos[k] = jnp.where(same, -1, pos[k])
-        whi, wlo = [], []
-        for k in range(slots):
-            hi = wgt[k].astype(BF).astype(F32)
-            whi.append(jnp.broadcast_to(hi, (step, LANE)).astype(BF))
-            wlo.append(jnp.broadcast_to(wgt[k] - hi, (step, LANE)).astype(BF))
-        for block in range(rows // 256):
-            loc = []
-            for k in range(slots):
-                local = pos[k] - block * 256
-                local = jnp.where((local >= 0) & (local < 256), local, -1).astype(F32)
-                loc.append(jnp.broadcast_to(local, (step, LANE)).astype(BF))
-            for part in range(256 // step):
-                row = (first + part * step).astype(BF)
-                hi = jnp.zeros((step, LANE), BF)
-                lo = jnp.zeros((step, LANE), BF)
-                for k in range(slots):
-                    here = row == loc[k]
-                    hi = jnp.where(here, whi[k], hi)
-                    lo = jnp.where(here, wlo[k], lo)
-                at = pl.ds(block * 256 + part * step, step)
-                hi_ref[at, lanes] = hi
-                lo_ref[at, lanes] = lo
+        build_tile(nbr_ref, w_ref, hi_ref, lo_ref, diag_ref, i, i)
         return 0
 
-    lax.fori_loop(0, lines, body, 0)
+    lax.fori_loop(0, cells // LANE, body, 0)
+    copies[2].wait()
+    fill_cat(cat_ref, x_ref, pair_ref, other_ref)
+    for c in range(cells // 256):
+        at = pl.ds(c * 256, 256)
+        y_ref[:, at] = diag_ref[:, at] * x_ref[:, at] + product(cat_ref, hi_ref, lo_ref, rows, at)
+    hi, lo = split(y_ref[...])
+    cat_ref[0:columns, 0:cells] = hi
+    cat_ref[columns:, 0:cells] = lo
+    for c in range(cells // 256):
+        at = pl.ds(c * 256, 256)
+        out_ref[:, at] = diag_ref[:, at] * y_ref[:, at] + product(cat_ref, hi_ref, lo_ref, cells, at)
 
 
 def params(mb):
@@ -86,20 +176,63 @@
     return [pl.BlockSpec(memory_space=VMEM)] * count
 
 
-def build(nbr, w, cells):
+HBM = pl.BlockSpec(memory_space=pltpu.HBM)
+
+
+def operator_shapes(cells):
     rows = cells + 2 * RIM
-    return pl.pallas_call(
-        build_kernel,
-        in_specs=whole(2),
-        out_specs=whole(3),
-        out_shape=[
-            jax.ShapeDtypeStruct((rows, cells), BF),
-            jax.ShapeDtypeStruct((rows, cells), BF),
-            jax.ShapeDtypeStruct((1, cells), F32),
+    return [
+        jax.ShapeDtypeStruct((rows, cells), BF),
+        jax.ShapeDtypeStruct((rows, cells), BF),
+        jax.ShapeDtypeStruct((1, cells), F32),
+    ]
+
+
+def pinned(*arrays):
+    return [pltpu.with_memory_space_constraint(x, pltpu.HBM) for x in arrays]
+
+
+def edge(nbr, w, x, low, high):
+    columns, cells = x.shape
+    rows = cells + 2 * RIM
+    return pl.pallas_call(
+        edge_kernel,
+        in_specs=[HBM] * 3 + whole(2),
+        out_specs=whole(2),
+        out_shape=[jax.ShapeDtypeStruct((columns, RIM), F32)] * 2,
+        scratch_shapes=[
+            VMEM(nbr.shape, nbr.dtype),
+            VMEM(w.shape, w.dtype),
+            VMEM((columns, cells), F32),
+            VMEM((rows, 2 * LANE), BF),
+            VMEM((rows, 2 * LANE), BF),
+            VMEM((1, 2 * LANE), F32),
+            VMEM((2 * columns, rows), BF),
+            pltpu.SemaphoreType.DMA((3,)),
         ],
         compiler_params=params(24),
-        name="build",
-    )(nbr, w)
+        name="edge",
+    )(*pinned(nbr, w, x), low, high)
+
+
+def main(nbr, w, x, low, high):
+    columns, cells = x.shape
+    return pl.pallas_call(
+        main_kernel,
+        in_specs=[HBM] * 3 + whole(2),
+        out_specs=whole(4),
+        out_shape=operator_shapes(cells) + [jax.ShapeDtypeStruct((columns, cells), F32)],
+        scratch_shapes=[
+            VMEM(nbr.shape, nbr.dtype),
+            VMEM(w.shape, w.dtype),
+            VMEM((columns, cells), F32),
+            VMEM((2 * columns, cells + 2 * RIM), BF),
+            VMEM((columns, cells), F32),
+            pltpu.SemaphoreType.DMA((3,)),
+        ],
+        compiler_params=params(24),
+        name="main",
+    )(*pinned(nbr, w, x), low, high)
 
 
 def own_kernel(x_ref, hi_ref, lo_ref, diag_ref, out_ref, cat_ref):
@@ -127,10 +260,11 @@
     )(x, a_hi, a_lo, diag)
 
 
-def rim_update(part_ref, low_ref, high_ref, hi_ref, lo_ref, c):
+def rim_update(part_ref, pair_ref, other_ref, hi_ref, lo_ref, c):
     columns, cells = part_ref.shape
-    lo_hi, lo_lo = split(low_ref[...])
-    hi_hi, hi_lo = split(high_ref[...])
+    low, high = sides(pair_ref, other_ref)
+    lo_hi, lo_lo = split(low)
+    hi_hi, hi_lo = split(high)
     top = jnp.concatenate([lo_hi, hi_hi], axis=1)
     rest = jnp.concatenate([lo_lo, hi_lo], axis=1)
     lanes = pl.ds(c * 256, 256)
@@ -139,15 +273,15 @@
     return part_ref[:, lanes] + (both[0:columns] + both[columns:] + dot(top, lo_ref[rows, lanes]))
 
 
-def rim_kernel(part_ref, low_ref, high_ref, hi_ref, lo_ref, out_ref, first_ref, last_ref):
+def rim_kernel(part_ref, pair_ref, other_ref, hi_ref, lo_ref, out_ref, pair_out, other_out):
     count = out_ref.shape[1] // 256
     for c in range(count):
-        out = rim_update(part_ref, low_ref, high_ref, hi_ref, lo_ref, c)
+        out = rim_update(part_ref, pair_ref, other_ref, hi_ref, lo_ref, c)
         out_ref[:, c * 256 : (c + 1) * 256] = out
         if c == 0:
-            first_ref[...] = out[:, 0:RIM]
+            first = out[:, 0:RIM]
         if c == count - 1:
-            last_ref[...] = out[:, 256 - RIM :]
+            send(first, out[:, 256 - RIM :], pair_out, other_out)
 
 
 def rim(part, low, high, a_hi, a_lo):
@@ -167,7 +301,7 @@
 
 
 def finish_kernel(
-    part_ref, low_ref, high_ref, hi_ref, lo_ref, remapped_ref, rate_ref, mix_ref,
+    part_ref, pair_ref, other_ref, hi_ref, lo_ref, remapped_ref, rate_ref, mix_ref,
     out_ref, copy_ref,
 ):
     fields, levels = mix_ref.shape[0], mix_ref.shape[1]
@@ -175,7 +309,7 @@
     row = lax.broadcasted_iota(jnp.int32, (levels, 256), 0)
     mixes = [split(mix_ref[f]) for f in range(fields)]
     for c in range(part_ref.shape[1] // 256):
-        mixed = rim_update(part_ref, low_ref, high_ref, hi_ref, lo_ref, c)
+        mixed = rim_update(part_ref, pair_ref, other_ref, hi_ref, lo_ref, c)
         at = pl.ds(c * 256, 256)
         for f in range(fields):
             mine = mixed[f * levels : (f + 1) * levels]
@@ -208,13 +342,26 @@
 
 
 def pack_kernel(
-    state_ref, source_ref, owner_ref, cell_ref, weight_ref, out_ref,
-    tiles_ref, slot_ref, owner_f_ref, piece_ref, hot_ref, rank_ref, left_ref, right_ref, acc_ref,
+    state_hbm, source_hbm, owner_hbm, cell_hbm, weight_hbm, out_ref,
+    state_ref, source_ref, owner_ref, cell_ref, weight_ref, sems,
+    tiles_ref, slot_ref, owner_f_ref, piece_ref, hot_ref, rank_ref, left_a, left_b, right_a, right_b, acc_ref,
 ):
+    copies = fetch(
+        (
+            (owner_hbm, owner_ref),
+            (source_hbm, source_ref),
+            (cell_hbm, cell_ref),
+            (weight_hbm, weight_ref),
+            (state_hbm.at[:, pl.ds(0, 8), :], state_ref),
+        ),
+        sems,
+    )
+    for copy in copies:
+        copy.wait()
     fields = state_ref.shape[0]
     rows = source_ref.shape[0]
     blocks = out_ref.shape[0] // 16
-    chunk = right_ref.shape[1]
+    chunk = right_a.shape[1]
     per = chunk // LANE
     groups = blocks // 2
     owner_f_ref[...] = owner_ref[...].astype(F32)
@@ -252,34 +399,31 @@
         slot_ref[r : r + 1, :] = jnp.sum(hot * (rank_ref[at, 0:LANE] + base), axis=0, keepdims=True)
         base = base + rank_ref[at, LANE:]
 
-    acc_ref[...] = jnp.zeros_like(acc_ref)
     eight = jnp.where(i16 < 8, 0.0, 1.0)
-
-    def body(c, _):
+    for c in range(rows // per):
+        left_ref, right_ref = ((left_a, right_a), (left_b, right_b))[c % 2]
         for t in range(per):
             r = c * per + t
             at = pl.ds(t * LANE, LANE)
-            one = pl.ds(r, 1)
-            tile = tiles_ref[pl.ds(pl.multiple_of(r * 8, 8), 8), :]
+            tile = tiles_ref[r * 8 : r * 8 + 8, :]
             tile = jnp.concatenate([tile, tile], axis=0).astype(BF)
-            owner = row16(owner_f_ref[one, :])
+            owner = row16(owner_f_ref[r : r + 1, :])
             who = (owner - eight).astype(BF)
             for o in range(groups):
                 left_ref[o * 16 : (o + 1) * 16, at] = jnp.where(who == 2 * o, tile, zero16)
             who = (owner - i16).astype(BF)
             for part in range(2):
-                piece = row16(piece_ref[pl.ds(part * rows + r, 1), :]).astype(BF)
+                piece = row16(piece_ref[part * rows + r : part * rows + r + 1, :]).astype(BF)
                 for o in range(blocks // 16):
                     top = groups * 16 + part * blocks + o * 16
                     left_ref[top : top + 16, at] = jnp.where(who == 16 * o, piece, zero16)
-            who = row16(slot_ref[one, :]).astype(BF)
+            who = row16(slot_ref[r : r + 1, :]).astype(BF)
             for o in range(2 * LANE // 16):
                 here = (i16 + o * 16).astype(BF) == who
                 right_ref[o * 16 : (o + 1) * 16, at] = jnp.where(here, one16, zero16)
-        acc_ref[...] += dot_nt(left_ref[...], right_ref[...])
-        return 0
-
-    lax.fori_loop(0, rows // per, body, 0)
+        more = dot_nt(left_ref[...], right_ref[...])
+        acc_ref[...] = more if c == 0 else acc_ref[...] + more
+
     low = lax.broadcasted_iota(jnp.int32, (8, LANE), 0) < 4
     for o in range(blocks):
         at = pl.ds(o * 8, 8)
@@ -298,14 +442,19 @@
 def pack(state, source, owner, cell, weight, blocks):
     fields, levels, cells = state.shape
     rows = source.shape[0]
-    chunk = 512
+    chunk = 1024
     return pl.pallas_call(
         pack_kernel,
-        grid=(1,),
-        in_specs=[pl.BlockSpec((fields, 8, cells), lambda i: (0, 0, 0))] + whole(4),
+        in_specs=[HBM] * 5,
         out_specs=whole(1)[0],
         out_shape=jax.ShapeDtypeStruct((blocks * 16, LANE), F32),
         scratch_shapes=[
+            VMEM((fields, 8, cells), F32),
+            VMEM((rows, LANE), jnp.int32),
+            VMEM((rows, LANE), jnp.int32),
+            VMEM((rows, LANE), jnp.int32),
+            VMEM((rows, LANE), F32),
+            pltpu.SemaphoreType.DMA((5,)),
             VMEM((rows * 2 * fields, LANE), F32),
             VMEM((rows, LANE), F32),
             VMEM((rows, LANE), F32),
@@ -313,29 +462,30 @@
             VMEM((rows * blocks, LANE), BF),
             VMEM((rows * blocks, 2 * LANE), F32),
             VMEM((blocks * 10, chunk), BF),
+            VMEM((blocks * 10, chunk), BF),
+            VMEM((2 * LANE, chunk), BF),
             VMEM((2 * LANE, chunk), BF),
             VMEM((blocks * 10, 2 * LANE), F32),
         ],
         compiler_params=params(20),
         name="pack",
-    )(state, source, owner, cell, weight)
+    )(*pinned(state, source, owner, cell, weight))
 
 
 def unpack_kernel(in_ref, out_ref, left_ref, right_ref):
     fields, cells = out_ref.shape
     blocks = in_ref.shape[0] // 16
     groups = cells // 256
-    chunk = right_ref.shape[1]
-    per = chunk // (2 * LANE)
     i16 = lax.broadcasted_iota(jnp.int32, (16, LANE), 0).astype(F32)
     eight = jnp.where(i16 < 8, 0.0, 1.0)
     one16 = jnp.ones((16, LANE), BF)
     zero16 = jnp.zeros((16, LANE), BF)
-
-    def body(c, acc):
+    per = 4
+
+    def body(c, _):
         for t in range(2 * per):
             top = pl.multiple_of((c * per + t // 2) * 16, 16)
-            at = pl.ds(t * LANE, LANE)
+            at = pl.ds(pl.multiple_of((c * 2 * per + t) * LANE, LANE), LANE)
             cell = in_ref[pl.ds(top + 8 + t % 2, 1), :].astype(jnp.int32)
             group = (cell // 256).astype(F32)
             local = row16((cell % 256).astype(F32)).astype(BF)
@@ -349,15 +499,16 @@
             for o in range(16):
                 here = (i16 + o * 16).astype(BF) == local
                 right_ref[o * 16 : (o + 1) * 16, at] = jnp.where(here, one16, zero16)
-        return acc + dot_nt(left_ref[...], right_ref[...])
-
-    acc = lax.fori_loop(0, blocks // per, body, jnp.zeros((groups * 8, 256), F32))
+        return 0
+
+    lax.fori_loop(0, blocks // per, body, 0)
+    acc = dot_nt(left_ref[...], right_ref[...])
     for g in range(groups):
         out_ref[:, g * 256 : (g + 1) * 256] = acc[g * 8 : g * 8 + 4] + acc[g * 8 + 4 : g * 8 + 8]
 
 
 def unpack(packed, fields, count):
-    chunk = 1024
+    chunk = packed.shape[0] // 8 * LANE
     return pl.pallas_call(
         unpack_kernel,
         in_specs=whole(1),
@@ -376,30 +527,32 @@
     fields, levels, cells = state.shape[1:]
     columns = fields * levels
     blocks = lax.axis_size("blk")
-    forward = [(i, (i + 1) % blocks) for i in range(blocks)]
-    backward = [(b, a) for a, b in forward]
+    pairs = [(i, i ^ 1) for i in range(blocks)]
+    others = [(i, (i + 1 if i % 2 else i - 1) % blocks) for i in range(blocks)]
 
     def lines(x):
         return x.reshape(-1, LANE)
 
-    def exchange(first, last):
-        low = lax.ppermute(last, "blk", forward)
-        high = lax.ppermute(first, "blk", backward)
-        return low, high
+    def exchange(to_pair, to_other):
+        return lax.ppermute(to_pair, "blk", pairs), lax.ppermute(to_other, "blk", others)
 
     x = state.reshape(columns, cells)
-    halo = exchange(x[:, :RIM], x[:, cells - RIM :])
+    nbr, weight = lines(neighbour), lines(edge_weight)
+    odd = lax.axis_index("blk") % 2 == 1
+    first, last = x[:, :RIM], x[:, cells - RIM :]
+    start = exchange(jnp.where(odd, first, last), jnp.where(odd, last, first))
     packed = pack(
         state[0], lines(remap_source), lines(remap_owner), lines(remap_cell),
         lines(remap_weight), blocks,
     )
     packed = lax.all_to_all(packed.reshape(blocks, 16, LANE), "blk", 0, 0, tiled=True)
-    a_hi, a_lo, diag = build(lines(neighbour), lines(edge_weight), cells)
-    for step in range(SUB - 1):
+    halo = exchange(*edge(nbr, weight, x, *start))
+    packed, nbr = lax.optimization_barrier((packed, nbr))
+    a_hi, a_lo, diag, part = main(nbr, weight, x, *start)
+    for step in range(1, SUB - 1):
+        x, *ends = rim(part, *halo, a_hi, a_lo)
+        halo = exchange(*ends)
         part = own(x, a_hi, a_lo, diag)
-        x, first, last = rim(part, *halo, a_hi, a_lo)
-        halo = exchange(first, last)
-    part = own(x, a_hi, a_lo, diag)
     partial_sum = unpack(packed.reshape(blocks * 16, LANE), fields, cells)
     remapped = lax.ppermute(partial_sum, "sec", [(0, 1), (1, 0)])
     out, remapped = finish(part, *halo, a_hi, a_lo, remapped, coupling_rate[0], vertical_mix[0])

time: 97.6 us -> 82.5 us (0.85)
  local copies, waits for them, and re-layouts: 15.3 us -> 0.01 us
  starting transfers between devices: 42.9 us -> 32.5 us
  waiting for transfers between devices: 0.03 us -> 7.07 us
  Pallas kernels: 37.8 us -> 41 us
    unnamed x28 -> x4, local copies, waits for them, and re-layouts: 14.5 us -> 0.01 us
    ppermute x8, starting transfers between devices: 27.7 us -> 18.1 us  [the longest x4 17.8 us: exchange(): lax.ppermute(to_other, 'blk', others)]
    pallas_call x2 -> x3, Pallas kernels: 17 us -> 25.7 us  [the longest x1 14.7 us: main(): pl.pallas_call(main_kernel, in_specs=[HBM] * 3 + whole(2), out_specs=whol...]
    ppermute x8, waiting for transfers between devices: 0.02 us -> 7.06 us  [the longest x4 7.05 us: exchange(): lax.ppermute(to_other, 'blk', others)]
    pallas_call x4 -> x2, Pallas kernels: 11 us -> 5.46 us  [own(): pl.pallas_call(own_kernel, in_specs=whole(4), out_specs=whole(1)[0], out_...]
  transfers between devices with their start and end apart: 10 -> 10, of which waited for: 0 -> 2; matrix products, arithmetic and copies ran while one was open for 1% -> 1% of each run, Pallas kernels for 27% -> 36%
where the time goes in v3:
time: 82.5 us; the launch traced here: 82.2 us
  Pallas kernels  41 us (50%)
  starting transfers between devices  32.5 us (39%)
  waiting for transfers between devices  7.07 us (9%)
    ppermute x4, starting transfers between devices, exchange(): lax.ppermute(to_other, 'blk', others)  17.8 us
    pallas_call x1, Pallas kernels, main(): pl.pallas_call(main_kernel, in_specs=[HBM] * 3 + whole(2), out_specs=whol...  14.7 us
    all_to_all x1, starting transfers between devices, per_device(): lax.all_to_all(packed.reshape(blocks, 16, LANE), 'blk', 0, 0, tiled=True)  12 us
    pallas_call x1, Pallas kernels, pack(): pl.pallas_call(pack_kernel, in_specs=[HBM] * 5, out_specs=whole(1)[0], ou...  8.49 us
    ppermute x4, waiting for transfers between devices, exchange(): lax.ppermute(to_other, 'blk', others)  7.05 us
    pallas_call x1, Pallas kernels, unpack(): pl.pallas_call(unpack_kernel, in_specs=whole(1), out_specs=whole(1)[0], o...  6.08 us
    pallas_call x2, Pallas kernels, own(): pl.pallas_call(own_kernel, in_specs=whole(4), out_specs=whole(1)[0], out_...  5.46 us
    pallas_call x1, Pallas kernels, finish(): pl.pallas_call(finish_kernel, in_specs=whole(8), out_specs=whole(2), out_...  2.82 us
  transfers between devices with their start and end apart: 10, of which 2 were waited for; matrix products, arithmetic and copies ran while one was open for 1% of the time, Pallas kernels for 36%

profile of v3, /device:TPU:1, one launch (start us, length us, event | category | flops | bytes accessed | tf_op | source)
XLA Modules:
  0.0 82.2 jit_solution(10249551337110942425)
XLA Ops:
  0.6 8.5 %pack.1 = f32[1024,128]{1,0:T(8,128)} custom-call(f32[4,16,2048]{2,1,0:T(8,128)} %bitcast.17, s32[64,128]{1,0:T(8,128)} %bitcast.25, s32[64,128]{1,0:T(8,128)} %bitcast.26, s32[64,128]{1,0:T(8,128)} %bitcast.27, f32[64,128]{1,0:T(8,128)} %bitcast.28), custom_call_target="tpu_custom_call" | custom-call | tf_op jit(solution)/shard_map/pack/pallas_call | solution.py:446
  9.1 12.0 %all-to-all-start = ((f32[64,16,128]{2,1,0:T(8,128)}), f32[64,16,128]{2,1,0:T(8,128)S(1)}, u32[]{:S(2)}, u32[]{:S(2)}) async-start(f32[64,16,128]{2,1,0:T(8,128)} %bitcast.5), calls=%async_computation | async-start | bytes 1048576 | tf_op jit(solution)/shard_map/all_to_all | solution.py:548
  21.1 0.8 slice_select_fusion
  21.9 6.8 %collective-permute-start.1 = (f32[64,128]{1,0:T(8,128)S(1)}, f32[64,128]{1,0:T(8,128)S(1)}, u32[]{:S(2)}, u32[]{:S(2)}) collective-permute-start(f32[64,128]{1,0:T(8,128)S(1)} %get-tuple-element.34), channel_id=1, source_target_pairs={{0,63},{1,2},{2,1},{3,4},{4,3},{5,6},{6,5},{7,8},{8,7},{9,10},{10,... | collective-permute-start | bytes 98312 | tf_op jit(solution)/shard_map/ppermute | solution.py:537
  28.7 0.0 collective-permute-start
  28.7 5.2 %collective-permute-done.1.other_ref = f32[64,128]{1,0:T(8,128)S(1)} collective-permute-done((f32[64,128]{1,0:T(8,128)S(1)}, f32[64,128]{1,0:T(8,128)S(1)}, u32[]{:S(2)}, u32[]{:S(2)}) %collective-permute-start.1) | collective-permute-done | bytes 32800 | tf_op jit(solution)/shard_map/ppermute | solution.py:537
  33.8 2.5 %edge.1 = (f32[64,128]{1,0:T(8,128)S(1)}, f32[64,128]{1,0:T(8,128)S(1)}) custom-call(s32[96,128]{1,0:T(8,128)} %bitcast.21, f32[96,128]{1,0:T(8,128)} %bitcast.23, f32[64,2048]{1,0:T(8,128)} %bitcast.19, f32[64,128]{1,0:T(8,128)S(1)} %collective-permute-done.pair_ref, f32[64,128]{1,0:T(8,128)S(1)} %collective-permute-done.1.other_ref), custom_call_target="tpu_custom_call" | custom-call | tf_op jit(solution)/shard_map/edge/pallas_call | solution.py:198
  36.4 0.1 collective-permute-start.2
  36.5 3.3 %collective-permute-start.3 = (f32[64,128]{1,0:T(8,128)S(1)}, f32[64,128]{1,0:T(8,128)S(1)}, u32[]{:S(2)}, u32[]{:S(2)}) collective-permute-start(f32[64,128]{1,0:T(8,128)S(1)} %get-tuple-element.21), channel_id=1, source_target_pairs={{0,63},{1,2},{2,1},{3,4},{4,3},{5,6},{6,5},{7,8},{8,7},{9,10},{10,... | collective-permute-start | bytes 98312 | tf_op jit(solution)/shard_map/ppermute | solution.py:537
  39.7 0.0 all-to-all-done
  39.7 14.7 %main.1 = (bf16[2304,2048]{1,0:T(8,128)(2,1)S(1)}, bf16[2304,2048]{1,0:T(8,128)(2,1)S(1)}, f32[1,2048]{1,0:T(1,128)S(1)}, f32[64,2048]{1,0:T(8,128)S(1)}) custom-call(s32[96,128]{1,0:T(8,128)} %bitcast.22, f32[96,128]{1,0:T(8,128)} %bitcast.24, f32[64,2048]{1,0:T(8,128)} %bitcast.20, f32[64,128]{1,0:T(8,128)S(1)} %collective-permute-done.pair_ref, ...), custom_call_target="tpu_custom_call" | custom-call | tf_op jit(solution)/shard_map/main/pallas_call | solution.py:220
  54.4 0.0 collective-permute-done.2.pair_ref
  54.4 0.5 rim.2
  54.9 0.1 collective-permute-start.4
  55.0 4.0 %collective-permute-start.5 = (f32[64,128]{1,0:T(8,128)S(1)}, f32[64,128]{1,0:T(8,128)S(1)}, u32[]{:S(2)}, u32[]{:S(2)}) collective-permute-start(f32[64,128]{1,0:T(8,128)S(1)} %get-tuple-element.27), channel_id=1, source_target_pairs={{0,63},{1,2},{2,1},{3,4},{4,3},{5,6},{6,5},{7,8},{8,7},{9,10},{10,... | collective-permute-start | bytes 98312 | tf_op jit(solution)/shard_map/ppermute | solution.py:537
  59.0 6.1 %unpack.1 = f32[4,2048]{1,0:T(4,128)S(1)} custom-call(f32[1024,128]{1,0:T(8,128)S(1)} %bitcast.14), custom_call_target="tpu_custom_call" | custom-call | tf_op jit(solution)/shard_map/unpack/pallas_call | solution.py:512
  65.1 2.5 %collective-permute-start.8 = (f32[4,2048]{1,0:T(4,128)S(1)}, f32[4,2048]{1,0:T(4,128)S(1)}, u32[]{:S(2)}, u32[]{:S(2)}) collective-permute-start(f32[4,2048]{1,0:T(4,128)S(1)} %unpack.1), channel_id=1, source_target_pairs={{0,64},{64,0},{1,65},{65,1},{2,66},{66,2},{3,67},{67,3},{4,68},{68... | collective-permute-start | bytes 98312 | tf_op jit(solution)/shard_map/ppermute | solution.py:557
  67.5 2.7 %own.2.part_ref = f32[64,2048]{1,0:T(8,128)S(1)} custom-call(f32[64,2048]{1,0:T(8,128)S(1)} %get-tuple-element.24.x_ref, bf16[2304,2048]{1,0:T(8,128)(2,1)S(1)} %get-tuple-element.22.hi_ref, bf16[2304,2048]{1,0:T(8,128)(2,1)S(1)} %get-tuple-element.23.lo_ref, f32[1,2048]{1,0:T(1,128)S(1)} %get-tuple-element.25.diag_ref), custom_call_target="tpu_custom_call" | custom-call | tf_op jit(solution)/shard_map/own/pallas_call | solution.py:252
  70.3 0.5 rim.3
  70.8 0.1 collective-permute-start.6
  70.9 3.9 %collective-permute-start.7 = (f32[64,128]{1,0:T(8,128)S(1)}, f32[64,128]{1,0:T(8,128)S(1)}, u32[]{:S(2)}, u32[]{:S(2)}) collective-permute-start(f32[64,128]{1,0:T(8,128)S(1)} %get-tuple-element.30), channel_id=1, source_target_pairs={{0,63},{1,2},{2,1},{3,4},{4,3},{5,6},{6,5},{7,8},{8,7},{9,10},{10,... | collective-permute-start | bytes 98312 | tf_op jit(solution)/shard_map/ppermute | solution.py:537
  74.7 2.7 %own.3.part_ref = f32[64,2048]{1,0:T(8,128)S(1)} custom-call(f32[64,2048]{1,0:T(8,128)S(1)} %get-tuple-element.28.x_ref, bf16[2304,2048]{1,0:T(8,128)(2,1)S(1)} %get-tuple-element.22.hi_ref, bf16[2304,2048]{1,0:T(8,128)(2,1)S(1)} %get-tuple-element.23.lo_ref, f32[1,2048]{1,0:T(1,128)S(1)} %get-tuple-element.25.diag_ref), custom_call_target="tpu_custom_call" | custom-call | tf_op jit(solution)/shard_map/own/pallas_call | solution.py:252
  77.5 1.9 %collective-permute-done.7.other_ref = f32[64,128]{1,0:T(8,128)S(1)} collective-permute-done((f32[64,128]{1,0:T(8,128)S(1)}, f32[64,128]{1,0:T(8,128)S(1)}, u32[]{:S(2)}, u32[]{:S(2)}) %collective-permute-start.7) | collective-permute-done | bytes 32800 | tf_op jit(solution)/shard_map/ppermute | solution.py:537
  79.4 2.8 %finish.1 = (f32[4,16,2048]{2,1,0:T(8,128)}, f32[4,2048]{1,0:T(4,128)}) custom-call(f32[64,2048]{1,0:T(8,128)S(1)} %own.3.part_ref, f32[64,128]{1,0:T(8,128)S(1)} %collective-permute-done.6.pair_ref, f32[64,128]{1,0:T(8,128)S(1)} %collective-permute-done.7.other_ref, bf16[2304,2048]{1,0:T(8,128)(2,1)S(1)} %get-tuple-element.22.hi_ref, ...), custom_call_target="tpu_custom_call" | custom-call | tf_op jit(solution)/shard_map/finish/pallas_call | solution.py:327
  (10 shorter events, 0.0 us)
Async XLA Ops:
  9.1 30.6 %all-to-all-start = ((f32[64,16,128]{2,1,0:T(8,128)}), f32[64,16,128]{2,1,0:T(8,128)S(1)}, u32[]{:S(2)}, u32[]{:S(2)}) async-start(f32[64,16,128]{2,1,0:T(8,128)} %bitcast.5), calls=%async_computation | async-start | bytes 1048576 | tf_op jit(solution)/shard_map/all_to_all | solution.py:548
  21.9 11.9 %collective-permute-start.1 = (f32[64,128]{1,0:T(8,128)S(1)}, f32[64,128]{1,0:T(8,128)S(1)}, u32[]{:S(2)}, u32[]{:S(2)}) collective-permute-start(f32[64,128]{1,0:T(8,128)S(1)} %get-tuple-element.34), channel_id=1, source_target_pairs={{0,63},{1,2},{2,1},{3,4},{4,3},{5,6},{6,5},{7,8},{8,7},{9,10},{10,... | collective-permute-start | bytes 98312 | tf_op jit(solution)/shard_map/ppermute | solution.py:537
  28.7 5.2 %collective-permute-start = (f32[64,128]{1,0:T(8,128)S(1)}, f32[64,128]{1,0:T(8,128)S(1)}, u32[]{:S(2)}, u32[]{:S(2)}) collective-permute-start(f32[64,128]{1,0:T(8,128)S(1)} %get-tuple-element.35), channel_id=1, source_target_pairs={{0,1},{1,0},{2,3},{3,2},{4,5},{5,4},{6,7},{7,6},{8,9},{9,8},{10,11... | collective-permute-start | bytes 98312 | tf_op jit(solution)/shard_map/ppermute | solution.py:537
  36.4 18.1 %collective-permute-start.2 = (f32[64,128]{1,0:T(8,128)S(1)}, f32[64,128]{1,0:T(8,128)S(1)}, u32[]{:S(2)}, u32[]{:S(2)}) collective-permute-start(f32[64,128]{1,0:T(8,128)S(1)} %get-tuple-element.20), channel_id=1, source_target_pairs={{0,1},{1,0},{2,3},{3,2},{4,5},{5,4},{6,7},{7,6},{8,9},{9,8},{10,11... | collective-permute-start | bytes 98312 | tf_op jit(solution)/shard_map/ppermute | solution.py:537
  36.5 18.0 %collective-permute-start.3 = (f32[64,128]{1,0:T(8,128)S(1)}, f32[64,128]{1,0:T(8,128)S(1)}, u32[]{:S(2)}, u32[]{:S(2)}) collective-permute-start(f32[64,128]{1,0:T(8,128)S(1)} %get-tuple-element.21), channel_id=1, source_target_pairs={{0,63},{1,2},{2,1},{3,4},{4,3},{5,6},{6,5},{7,8},{8,7},{9,10},{10,... | collective-permute-start | bytes 98312 | tf_op jit(solution)/shard_map/ppermute | solution.py:537
  54.9 15.3 %collective-permute-start.4 = (f32[64,128]{1,0:T(8,128)S(1)}, f32[64,128]{1,0:T(8,128)S(1)}, u32[]{:S(2)}, u32[]{:S(2)}) collective-permute-start(f32[64,128]{1,0:T(8,128)S(1)} %get-tuple-element.26), channel_id=1, source_target_pairs={{0,1},{1,0},{2,3},{3,2},{4,5},{5,4},{6,7},{7,6},{8,9},{9,8},{10,11... | collective-permute-start | bytes 98312 | tf_op jit(solution)/shard_map/ppermute | solution.py:537
  55.0 15.3 %collective-permute-start.5 = (f32[64,128]{1,0:T(8,128)S(1)}, f32[64,128]{1,0:T(8,128)S(1)}, u32[]{:S(2)}, u32[]{:S(2)}) collective-permute-start(f32[64,128]{1,0:T(8,128)S(1)} %get-tuple-element.27), channel_id=1, source_target_pairs={{0,63},{1,2},{2,1},{3,4},{4,3},{5,6},{6,5},{7,8},{8,7},{9,10},{10,... | collective-permute-start | bytes 98312 | tf_op jit(solution)/shard_map/ppermute | solution.py:537
  65.1 12.4 %collective-permute-start.8 = (f32[4,2048]{1,0:T(4,128)S(1)}, f32[4,2048]{1,0:T(4,128)S(1)}, u32[]{:S(2)}, u32[]{:S(2)}) collective-permute-start(f32[4,2048]{1,0:T(4,128)S(1)} %unpack.1), channel_id=1, source_target_pairs={{0,64},{64,0},{1,65},{65,1},{2,66},{66,2},{3,67},{67,3},{4,68},{68... | collective-permute-start | bytes 98312 | tf_op jit(solution)/shard_map/ppermute | solution.py:557
  70.8 6.7 %collective-permute-start.6 = (f32[64,128]{1,0:T(8,128)S(1)}, f32[64,128]{1,0:T(8,128)S(1)}, u32[]{:S(2)}, u32[]{:S(2)}) collective-permute-start(f32[64,128]{1,0:T(8,128)S(1)} %get-tuple-element.29), channel_id=1, source_target_pairs={{0,1},{1,0},{2,3},{3,2},{4,5},{5,4},{6,7},{7,6},{8,9},{9,8},{10,11... | collective-permute-start | bytes 98312 | tf_op jit(solution)/shard_map/ppermute | solution.py:537
  70.9 8.5 %collective-permute-start.7 = (f32[64,128]{1,0:T(8,128)S(1)}, f32[64,128]{1,0:T(8,128)S(1)}, u32[]{:S(2)}, u32[]{:S(2)}) collective-permute-start(f32[64,128]{1,0:T(8,128)S(1)} %get-tuple-element.30), channel_id=1, source_target_pairs={{0,63},{1,2},{2,1},{3,4},{4,3},{5,6},{6,5},{7,8},{8,7},{9,10},{10,... | collective-permute-start | bytes 98312 | tf_op jit(solution)/shard_map/ppermute | solution.py:537
  74.7 4.6 %copy-start = (f32[1,4,2048]{2,1,0:T(4,128)S(1)}, f32[1,4,2048]{2,1,0:T(4,128)}, u32[]{:S(2)}) copy-start(f32[1,4,2048]{2,1,0:T(4,128)} %param.12) | copy-start | bytes 98308
  74.7 4.6 %copy-start.1 = (f32[1,4,16,16]{3,2,1,0:T(8,128)S(1)}, f32[1,4,16,16]{3,2,1,0:T(8,128)}, u32[]{:S(2)}) copy-start(f32[1,4,16,16]{3,2,1,0:T(8,128)} %param.13) | copy-start | bytes 12292
